TPU v7x, 32 devices: a whole 2x2x4 slice. The times are simulated.
32 devices in a mesh: gx: 4 (over y, core), gy: 4 (over z), frame: 2 (over x).
Axes of the slice: x: 2, y: 2, z: 4, core: 2. Of those that a mesh axis runs over, the one named last changes fastest.
Arguments:
- features: bfloat16 [8, 8, 128, 128], P(('frame', 'gx'), 'gy'), parts along dimension 0, may hold values from -6 to 6
- positions: float32 [8, 8, 3, 128], P(('frame', 'gx'), 'gy'), parts along dimension 0, may hold values from 0 to 1
- bead_types: int32 [8, 8, 128], P(('frame', 'gx'), 'gy'), parts along dimension 0, may hold values from 0 to 15
- cell_counts: int32 [8, 8], P(('frame', 'gx'), 'gy'), parts along dimension 0, may hold values from 48 to 128
- w_value: bfloat16 [128, 128], replicated, may hold values from -0.5 to 0.5
- w_radial: float32 [8, 128], replicated, may hold values from -0.6 to 0.6
- type_gain: float32 [16, 128], replicated, may hold values from 0.1 to 1.9
- w_out: bfloat16 [128, 128], replicated, may hold values from -0.5 to 0.5
- cotangent: bfloat16 [8, 8, 128, 128], P(('frame', 'gx'), 'gy'), parts along dimension 0, may hold values from -6 to 6
Outputs:
- out_feat: bfloat16 [8, 8, 128, 128], P(('frame', 'gx'), 'gy'), parts along dimension 0
- grad_feat: bfloat16 [8, 8, 128, 128], P(('frame', 'gx'), 'gy'), parts along dimension 0
- grad_pos: float32 [8, 8, 3, 128], P(('frame', 'gx'), 'gy'), parts along dimension 0
- grad_wvalue: float32 [256, 128], P('frame'), parts along dimension 0
- grad_wradial: float32 [16, 128], P('frame'), parts along dimension 0
- grad_gain: float32 [32, 128], P('frame'), parts along dimension 0
- grad_wout: float32 [256, 128], P('frame'), parts along dimension 0
There are 2 independent parts, one for each index of `frame`. A program takes and returns all parts, laid end to end along the dimension named above; an argument that names none is the same for every part. Nothing has to cross between parts.
All inputs are finite; a program needn't handle non-finite values.
Results may differ from a plain program's by a relative error of at most 0.012.
Values may be sent and summed in bfloat16 or wider, within the bound.
No kernel may reach another device: no remote copies, remote signals or barrier semaphores. Data moves between devices by JAX's collectives and lax.ppermute only.
A program may use at most 64 MiB of HBM per device.

v0:
```python
import functools
import math

import jax
import jax.numpy as jnp
from jax import lax
from jax.experimental import pallas as pl
from jax.experimental.pallas import tpu as pltpu
from jax.sharding import PartitionSpec as P


HZ = 6
SOFTEN = 0.01
FAR = 1024.0
AUX = 16
STRIP = 32
LANES = 128
LOG2E = math.log2(math.e)


f32 = jnp.float32
bf16 = jnp.bfloat16


def split3(x):
    hi = x.astype(bf16)
    rest = x - hi.astype(f32)
    mid = rest.astype(bf16)
    low = (rest - mid.astype(f32)).astype(bf16)
    return hi, mid, low


def dot(a, b):
    return jnp.dot(a, b, preferred_element_type=f32)


def dot_t(a, b):
    return lax.dot_general(a, b, (((1,), (1,)), ((), ())), preferred_element_type=f32)


def identity(size):
    rows = lax.broadcasted_iota(jnp.int32, (size, size), 0)
    lanes = lax.broadcasted_iota(jnp.int32, (size, size), 1)
    return jnp.where(rows == lanes, 1.0, 0.0).astype(bf16)


def gain_columns(type_gain):
    parts = [part.astype(f32) for part in split3(type_gain[...])]
    count, channels = type_gain.shape
    rows = jnp.concatenate(parts + [jnp.zeros((channels - 3 * count, channels), f32)], axis=0)
    return rows.T[:, 0 : 3 * count].astype(bf16)


def onehot_rows(types_row, type_count, slots):
    rows = lax.broadcasted_iota(jnp.int32, (3 * type_count, slots), 0)
    hit = (rows == types_row) | (rows == types_row + type_count) | (rows == types_row + 2 * type_count)
    return jnp.where(hit, 1.0, 0.0).astype(bf16)


def pack_kernel(
    order, counts, feat, pos, types, cotangent, w_value, w_radial, type_gain, w_out,
    packed, types_out, cotangent_out, w_value_out, w_radial_out, type_gain_out, w_out_out,
    counts_here, pos_here, sems,
):
    slots = feat.shape[2]
    moves = [(counts, counts_here), (pos, pos_here), (types, types_out)]
    for place in range(2):
        cell = jnp.where(order[1] == 0, place, 1 - place)
        moves.append((feat.at[0, cell], packed.at[place, 0:slots, :]))
    moves += [
        (w_value, w_value_out), (type_gain, type_gain_out), (cotangent, cotangent_out),
        (w_radial, w_radial_out), (w_out, w_out_out),
    ]
    copies = [pltpu.make_async_copy(a, b, sems.at[i]) for i, (a, b) in enumerate(moves)]
    for copy in copies:
        copy.start()
    for copy in copies[:3]:
        copy.wait()
    for place in range(2):
        cell = jnp.where(order[1] == 0, place, 1 - place)
        lane = lax.broadcasted_iota(jnp.int32, (1, slots), 1)
        valid = lane < counts_here[0, cell]
        parts = [[], [], []]
        for comp in range(3):
            row = pos_here[0, comp, pl.ds(cell, 1), :]
            if comp == 2:
                row = row * float(HZ)
            row = jnp.where(valid, row, -FAR)
            for which, part in enumerate(split3(row)):
                parts[which].append(part.astype(f32))
        rows = parts[0] + parts[1] + parts[2]
        rows.append(types_out[0, pl.ds(cell, 1), :].astype(f32))
        rows.append(jnp.zeros((AUX - len(rows), slots), f32))
        packed[place, slots : slots + AUX, :] = jnp.concatenate(rows, axis=0).astype(bf16)
    for copy in copies[3:]:
        copy.wait()


def pair_terms(near_pos, index, own_xyz, is_self, first_row, basis_count):
    n1 = float(basis_count - 1)
    gamma = 0.5 * n1 * n1
    delta = [near_pos[index, comp : comp + 1, :] - own_xyz[comp] for comp in range(3)]
    dist_sq = delta[0] * delta[0] + delta[1] * delta[1] + delta[2] * delta[2]
    dist_sq = jnp.minimum(dist_sq, 1.0)
    inside = 1.0 - dist_sq
    radius_sq = dist_sq + SOFTEN
    inverse = lax.rsqrt(radius_sq)
    radius = radius_sq * inverse
    gauss = jnp.exp2(radius_sq * (-gamma * LOG2E))
    step = jnp.exp2(radius * (n1 * LOG2E))
    if is_self:
        rows = first_row + lax.broadcasted_iota(jnp.int32, gauss.shape, 0)
        lanes = lax.broadcasted_iota(jnp.int32, gauss.shape, 1)
        gauss = jnp.where(rows == lanes, 0.0, gauss)
    part = inside * gauss
    weight = inside * part
    value_factor = part * (inside * -n1 - 2.0 * n1 / gamma)
    slope_factor = weight * (inverse * step)
    return step, weight, value_factor, slope_factor


def near_cell(aux, row, col, order):
    sx = jnp.where(order[0] == 0, 1.0, -1.0).astype(f32)
    sy = jnp.where(order[1] == 0, 1.0, -1.0).astype(f32)
    aux = aux.astype(f32)
    xyz = aux[0:3] + aux[3:6] + aux[6:9]
    x = xyz[0:1] + sx * float(1 - row)
    y = xyz[1:2] + sy * float(col)
    return [x, y, xyz[2:3]], xyz[0:1] < -0.5 * FAR, aux[9:10].astype(jnp.int32)


def strip_of(s):
    first = pl.multiple_of(s * STRIP, STRIP)
    return first, pl.ds(first, STRIP)


def stage(count, *steps):
    def body(s, carry):
        for step in steps:
            step(s)
        return carry

    lax.fori_loop(0, count, body, 0)


def fill_pairs(basis_count, slots, near_pos, own_pos, place, self_block, terms, weights, s):
    first, strip = strip_of(s)
    own_xyz = [own_pos[place, comp, strip, :] for comp in range(3)]
    for block in range(weights.shape[1] // slots):
        there = slice(block * slots, (block + 1) * slots)
        step, weight, value_factor, slope_factor = pair_terms(
            near_pos, block, own_xyz, block == self_block, first, basis_count
        )
        terms[0, strip, there] = step
        terms[1, strip, there] = value_factor
        terms[2, strip, there] = slope_factor
        for k in range(basis_count):
            rows = pl.ds(pl.multiple_of(first + k * slots, STRIP), STRIP)
            weights[rows, there] = weight.astype(bf16)
            if k < basis_count - 1:
                weight = weight * step


def carry_values(slots, value_t, gain_t, eye, near, here):
    near_feat, near_val, carried_t, onehot, projected, gains = near
    proj = dot_t(value_t, near_feat[here, :])
    gain = dot(gain_t, onehot[:, here])
    projected[:, here] = proj
    gains[:, here] = gain
    carried = (proj * gain).astype(bf16)
    carried_t[:, here] = carried
    for first in range(here.start, here.stop, slots):
        there = slice(first - here.start, first - here.start + slots)
        near_val[first : first + slots, :] = dot_t(eye, carried[:, there]).astype(bf16)


def chunk_of(s, size):
    return pl.ds(pl.multiple_of(s * size, size), size)


def early_kernel(
    basis_count, order, own, row_a, row_b, w_value, type_gain,
    near_pos, own_pos, near_feat, near_val, carried_t, onehot, projected, gains,
    weights_b, weights_a, terms_b, terms_a, summed_b, summed_a,
):
    slots = near_feat.shape[1]
    strips = slots // STRIP
    chunk = basis_count * slots // strips
    weights, terms, summed = (weights_b, weights_a), (terms_b, terms_a), (summed_b, summed_a)
    for index in range(6):
        col, row = index // 3 + 1, index % 3
        ref = (row_a, own, row_b)[row]
        here = slice(index * slots, (index + 1) * slots)
        near_feat[here, :] = ref[col - 1, 0:slots, :]
        xyz, unused, types = near_cell(ref[col - 1, slots : slots + AUX, :], row, col, order)
        onehot[:, here] = onehot_rows(types, type_gain.shape[0], slots)
        for comp in range(3):
            near_pos[index, comp : comp + 1, :] = xyz[comp]
            if row == 1:
                line = jnp.where(unused, FAR, xyz[comp])
                own_pos[col - 1, comp] = jnp.broadcast_to(line, (slots, slots)).T
    near = (near_feat, near_val, carried_t, onehot, projected, gains)
    value_t = w_value[...].astype(f32).T.astype(bf16)
    carry_values(slots, value_t, gain_columns(type_gain), identity(slots), near, slice(0, 6 * slots))

    def sums(place, s):
        rows = chunk_of(s, chunk)
        summed[place][:, rows] = dot_t(carried_t[...], weights[place][rows, :])

    def pairs(place, s):
        fill_pairs(
            basis_count, slots, near_pos, own_pos, place, 3 * place + 1, terms[place], weights[place], s
        )

    run = functools.partial
    stage(strips, run(pairs, 0))
    stage(strips, run(sums, 0), run(pairs, 1))
    stage(strips, run(sums, 1))


def main_kernel(
    basis_count, order, col_a, col_b, cotangent, w_value, w_radial, type_gain, w_out,
    in_pos, own_pos, in_feat, in_val, in_carried_t, in_onehot, in_projected, in_gains,
    in_weights_b, in_weights_a, in_terms_b, in_terms_a, in_summed_b, in_summed_a,
    out_feat, keep, pay_a, pay_b, fold_a, fold_b, own_acc,
    out_pos, ot_feat, ot_val, ot_carried_t, ot_onehot, ot_projected, ot_gains, columns, products, whole,
    ot_weights_b, ot_weights_a, ot_terms_b, ot_terms_a, summed_b, summed_a,
    scaled_b, scaled_a, scaled_tb, scaled_ta,
    in_grad_b, in_grad_a, ot_grad_b, ot_grad_a, in_back, ot_back, pull_own, pull_far,
):
    slots, channels = cotangent.shape[2], cotangent.shape[3]
    type_count = type_gain.shape[0]
    third = 3 * slots
    strips = slots // STRIP
    chunk = basis_count * slots // strips
    in_weights, ot_weights = (in_weights_b, in_weights_a), (ot_weights_b, ot_weights_a)
    in_terms, ot_terms = (in_terms_b, in_terms_a), (ot_terms_b, ot_terms_a)
    in_summed, summed = (in_summed_b, in_summed_a), (summed_b, summed_a)
    scaled, scaled_t = (scaled_b, scaled_a), (scaled_tb, scaled_ta)
    in_grad, ot_grad = (in_grad_b, in_grad_a), (ot_grad_b, ot_grad_a)
    for index in range(6):
        place, row = index // 3, index % 3
        ref = (col_b, col_a)[place]
        here = slice(index * slots, (index + 1) * slots)
        ot_feat[here, :] = ref[row, 0:slots, :]
        xyz, _, types = near_cell(ref[row, slots : slots + AUX, :], row, 3 * place, order)
        ot_onehot[:, here] = onehot_rows(types, type_count, slots)
        for comp in range(3):
            out_pos[index, comp : comp + 1, :] = xyz[comp]
    scale = [math.exp(-0.5 * k * k) for k in range(basis_count)]
    radial = [w_radial[k : k + 1, :] * scale[k] for k in range(basis_count)]
    radial_t = jnp.concatenate(radial + [jnp.zeros((channels - basis_count, channels), f32)], axis=0).T
    for k in range(basis_count):
        columns[k] = jnp.broadcast_to(radial_t[:, k : k + 1], (channels, slots))
    near = (ot_feat, ot_val, ot_carried_t, ot_onehot, ot_projected, ot_gains)
    value_t = w_value[...].astype(f32).T.astype(bf16)
    carry_values(slots, value_t, gain_columns(type_gain), identity(slots), near, slice(0, 6 * slots))

    def outer(place):
        return slice(place * third, (place + 1) * third)

    def pairs(place, s):
        cells = out_pos.at[place * 3 : place * 3 + 3]
        fill_pairs(basis_count, slots, cells, own_pos, place, -1, ot_terms[place], ot_weights[place], s)

    def sums(place, s):
        rows = chunk_of(s, chunk)
        summed[place][:, rows] = in_summed[place][:, rows] + dot_t(
            ot_carried_t[:, outer(place)], ot_weights[place][rows, :]
        )

    def epilogue(place):
        aggregate_t = None
        for k in range(basis_count):
            term = summed[place][:, k * slots : (k + 1) * slots] * columns[k]
            aggregate_t = term if aggregate_t is None else aggregate_t + term
        agg_half = aggregate_t.T.astype(bf16)
        cell = jnp.where(order[1] == 0, place, 1 - place)
        pre_act = dot(agg_half, w_out[...])
        sig = jax.nn.sigmoid(pre_act)
        center = in_feat[(3 * place + 1) * slots : (3 * place + 2) * slots, :]
        out_feat[0, cell] = (center.astype(f32) + pre_act * sig).astype(bf16)
        grad_pre = (
            cotangent[0, cell].astype(f32) * sig * (1.0 + pre_act * (1.0 - sig))
        ).astype(bf16)
        agg = dot_t(grad_pre, w_out[...]).astype(bf16).astype(f32)
        agg_t = agg.T
        for k in range(basis_count):
            here = slice(k * slots, (k + 1) * slots)
            scaled[place][here, :] = (agg * radial[k]).astype(bf16)
            scaled_t[place][:, here] = (agg_t * columns[k]).astype(bf16)
            product = agg_t * summed[place][:, here]
            products[:, here] = product if place == 0 else products[:, here] + product
        return dot(aggregate_t.astype(bf16), grad_pre)

    def weight_grads(place, s):
        rows = chunk_of(s, chunk)
        in_grad[place][rows, :] = dot_t(scaled[place][rows, :], in_val[...])
        ot_grad[place][rows, :] = dot_t(scaled[place][rows, :], ot_val[outer(place), :])

    def pulls(place, s):
        first, strip = strip_of(s)
        own_xyz = [own_pos[place, comp, strip, :] for comp in range(3)]
        total = [jnp.zeros((STRIP, slots), f32) for _ in range(3)]
        for block in range(9):
            inner = block < 6
            grad = (in_grad if inner else ot_grad)[place]
            terms = (in_terms if inner else ot_terms)[place]
            cells = in_pos if inner else out_pos
            cell = block if inner else place * 3 + block - 6
            index = block if inner else 6 + cell
            local = block if inner else block - 6
            there = slice(local * slots, (local + 1) * slots)

            def grad_of(k):
                rows = pl.ds(pl.multiple_of(first + k * slots, STRIP), STRIP)
                return grad[rows, there]

            step = terms[0, strip, there]
            value = grad_of(basis_count - 1)
            slope = None
            for k in range(basis_count - 2, -1, -1):
                slope = value if slope is None else value + step * slope
                value = grad_of(k) + step * value
            pull = terms[1, strip, there] * value + terms[2, strip, there] * slope
            for comp in range(3):
                force = pull * (cells[cell, comp : comp + 1, :] - own_xyz[comp])
                total[comp] = total[comp] + force
                pull_far[index, comp] += (force[0:8] + force[8:16]) + (force[16:24] + force[24:32])
        for comp in range(3):
            pull_own[place, comp, strip, :] = total[comp]

    def value_grads(s):
        rows = chunk_of(s, chunk)
        parts = [scaled_t[place][:, rows] for place in range(2)]
        in_back[...] += dot(parts[0], in_weights[0][rows, :]) + dot(parts[1], in_weights[1][rows, :])
        for place in range(2):
            ot_back[:, outer(place)] += dot(parts[place], ot_weights[place][rows, :])

    run = functools.partial
    pull_far[...] = jnp.zeros_like(pull_far)
    in_back[...] = jnp.zeros_like(in_back)
    ot_back[...] = jnp.zeros_like(ot_back)
    stage(strips, run(pairs, 0))
    stage(strips, run(sums, 0), run(pairs, 1))
    for s in range(strips):
        sums(1, s)
    wout = epilogue(0)
    for s in range(strips):
        weight_grads(0, s)
    wout = wout + epilogue(1)
    stage(strips, run(weight_grads, 1), run(pulls, 0))
    stage(strips, value_grads, run(pulls, 1))

    wvalue = ggain = None
    for back, feat, onehot, projected, gains in (
        (in_back, in_feat, in_onehot, in_projected, in_gains),
        (ot_back, ot_feat, ot_onehot, ot_projected, ot_gains),
    ):
        half = (back[...] * gains[...]).astype(bf16)
        hi, mid, _ = split3(back[...] * projected[...])
        wvalue_part = dot(half, feat[...])
        ggain_part = dot_t(hi, onehot[...]) + dot_t(mid, onehot[...])
        wvalue = wvalue_part if wvalue is None else wvalue + wvalue_part
        ggain = ggain_part if ggain is None else ggain + ggain_part
    ggain = jnp.concatenate([ggain, jnp.zeros((channels, slots - ggain.shape[1]), f32)], axis=1).T
    group = lax.broadcasted_iota(jnp.int32, (basis_count, basis_count * slots), 1) // slots
    mine = lax.broadcasted_iota(jnp.int32, (basis_count, basis_count * slots), 0)
    select = jnp.where(group == mine, 1.0, 0.0).astype(bf16)
    hi, mid, _ = split3(products[...])
    wradial = dot_t(select, hi) + dot_t(select, mid)
    wradial = jnp.concatenate([wradial[k : k + 1] * scale[k] for k in range(basis_count)], axis=0)
    pad = 2 * keep.shape[0] - 2 * channels - type_count - basis_count
    tail = [ggain[0:type_count], wradial] + ([jnp.zeros((pad, channels), f32)] if pad else [])
    full = jnp.concatenate([wvalue.T, wout] + tail, axis=0).astype(bf16)
    rows = keep.shape[0]
    whole[0] = full[0:rows]
    whole[1] = full[rows : 2 * rows]
    keep[...] = whole[order[0]]
    for ref in (pay_a, pay_b):
        ref[0:rows, :] = whole[1 - order[0]]
    force = float(basis_count - 1)
    size = slots + AUX
    for col in range(4):
        for row in range(3):
            inner = col in (1, 2)
            local = (col - 1) * 3 + row if inner else (0 if col == 0 else 3) + row
            back = (in_back if inner else ot_back)[:, local * slots : (local + 1) * slots]
            lines = []
            for comp in range(3):
                line = jnp.sum(pull_far[local if inner else 6 + local, comp], axis=0, keepdims=True)
                if row == 1 and inner:
                    line = line - jnp.sum(pull_own[col - 1, comp].T, axis=0, keepdims=True)
                lines.append(line * (force * HZ if comp == 2 else force))
            lines.append(jnp.zeros((AUX - 3, slots), f32))
            lines = jnp.concatenate(lines, axis=0)
            if row == 1:
                own_acc[col, 0:slots, :] = back
                own_acc[col, slots:size, :] = lines
                continue
            if inner:
                ref, base = (fold_a if row == 0 else fold_b), (col - 1) * size
            else:
                ref, base = (pay_a if row == 0 else pay_b), rows + (0 if col == 0 else size)
            ref[base : base + slots, :] = back.astype(bf16)
            ref[base + slots : base + size, :] = lines.astype(bf16)


def cell_grads(own, got_a, got_b, got, types_row, cotangent, w_value, type_gain):
    slots = cotangent.shape[0]
    total = own + (got_a.astype(f32) + got_b.astype(f32)) + got.astype(f32)
    gain = dot(gain_columns(type_gain), onehot_rows(types_row, type_gain.shape[0], slots))
    half = (total[0:slots] * gain).astype(bf16)
    feat = (cotangent.astype(f32) + dot(w_value[...], half).T).astype(bf16)
    return feat, total[slots : slots + 3]


def cells_kernel(
    order, own, got_a, got_b, far, near, types, cotangent, w_value, type_gain, grad_feat, grad_pos
):
    size = far.shape[0]
    for place in range(2):
        cell = jnp.where(order[1] == 0, place, 1 - place)
        here = slice(place * size, (place + 1) * size)
        got = far[...] if place == 0 else near[near.shape[0] - size :, :]
        feat, pos = cell_grads(
            own[place + 1], got_a[here, :], got_b[here, :], got, types[0, pl.ds(cell, 1), :],
            cotangent[0, cell], w_value, type_gain,
        )
        grad_feat[0, cell] = feat
        for comp in range(3):
            grad_pos[0, comp, pl.ds(cell, 1), :] = pos[comp : comp + 1]


def weights_kernel(order, mine, other, wvalue, wradial, ggain, wout):
    first = order[0] == 0
    low = jnp.where(first, mine[...], other[...])
    high = jnp.where(first, other[...], mine[...])
    total = jnp.concatenate([low, high], axis=0)
    base = 0
    for ref in (wvalue, wout, ggain, wradial):
        ref[...] = total[base : base + ref.shape[0]]
        base += ref.shape[0]


def edges(axis):
    count = lax.axis_size(axis)
    assert count % 2 == 0 and count > 2 and count & (count - 1) == 0
    even = [(i, i ^ 1) for i in range(count)]
    odd = [(i, (i + 1) % count if i % 2 else (i - 1) % count) for i in range(count)]
    return even, odd


def across(axis, step):
    return [(i, i ^ step) for i in range(lax.axis_size(axis))]


def add(a, b):
    return a.astype(f32) + b.astype(f32)


def on_device(
    features, positions, bead_types, cell_counts, w_value, w_radial, type_gain, w_out, cotangent
):
    row_count, col_count, slots, channels = features.shape
    basis_count, type_count = w_radial.shape[0], type_gain.shape[0]
    assert row_count == 1 and col_count == 2 and slots == channels == LANES
    assert 3 * type_count <= slots and type_count % 8 == 0 and basis_count == 8
    order = jnp.stack([lax.axis_index("gx") % 2, lax.axis_index("gy") % 2]).astype(jnp.int32)
    smem = pl.BlockSpec(memory_space=pltpu.SMEM)
    vmem = pl.BlockSpec(memory_space=pltpu.VMEM)
    x_even, x_odd = edges("gx")
    y_even, y_odd = edges("gy")
    size = slots + AUX
    inner, outer, tall = 6 * slots, 3 * slots, basis_count * slots
    rows = -(-(2 * channels + type_count + basis_count) // 32) * 16
    kinds = 3 * type_count
    shape = jax.ShapeDtypeStruct

    def call(kernel, mib, out_shape, arrays, scratch=()):
        return pl.pallas_call(
            kernel,
            out_shape=out_shape,
            in_specs=[smem] + [vmem] * len(arrays),
            out_specs=jax.tree.map(lambda _: vmem, out_shape),
            scratch_shapes=list(scratch),
            compiler_params=pltpu.CompilerParams(vmem_limit_bytes=mib * 2**20),
        )(order, *arrays)

    hbm = pl.BlockSpec(memory_space=pltpu.HBM)
    packed, bead_types, cotangent, w_value, w_radial, type_gain, w_out = pl.pallas_call(
        pack_kernel,
        out_shape=(
            shape((2, size, channels), bf16),
            *(shape(a.shape, a.dtype) for a in (bead_types, cotangent, w_value, w_radial, type_gain, w_out)),
        ),
        in_specs=[smem] + [hbm] * 9,
        out_specs=(vmem,) * 7,
        scratch_shapes=[
            pltpu.SMEM(cell_counts.shape, jnp.int32),
            pltpu.VMEM((row_count, 3, col_count, slots), f32),
            pltpu.SemaphoreType.DMA((10,)),
        ],
        compiler_params=pltpu.CompilerParams(vmem_limit_bytes=4 * 2**20),
        name="pack",
    )(
        order,
        *(
            pltpu.with_memory_space_constraint(a, pltpu.HBM)
            for a in (
                cell_counts, features, jnp.swapaxes(positions, 1, 2), bead_types, cotangent, w_value,
                w_radial, type_gain, w_out,
            )
        ),
    )
    row_b = lax.ppermute(packed, "gx", x_odd)
    row_a = lax.ppermute(packed, "gx", x_even)
    col_b = lax.ppermute(jnp.stack([row_a[0], packed[0], row_b[0]]), "gy", y_odd)
    col_a = lax.ppermute(jnp.stack([row_a[1], packed[1], row_b[1]]), "gy", y_even)
    early = call(
        functools.partial(early_kernel, basis_count), 8,
        (
            shape((6, 8, slots), f32),
            shape((2, 3, slots, slots), f32),
            shape((inner, channels), bf16),
            shape((inner, channels), bf16),
            shape((channels, inner), bf16),
            shape((kinds, inner), bf16),
            shape((channels, inner), f32),
            shape((channels, inner), f32),
        )
        + (shape((tall, inner), bf16),) * 2
        + (shape((3, slots, inner), f32),) * 2
        + (shape((channels, tall), f32),) * 2,
        (packed, row_a, row_b, w_value, type_gain),
    )
    out_feat, keep, pay_a, pay_b, fold_a, fold_b, own_acc = call(
        functools.partial(main_kernel, basis_count), 28,
        (
            shape(features.shape, bf16),
            shape((rows, channels), bf16),
            shape((rows + 2 * size, channels), bf16),
            shape((rows + 2 * size, channels), bf16),
            shape((2 * size, channels), bf16),
            shape((2 * size, channels), bf16),
            shape((4, size, slots), f32),
        ),
        (col_a, col_b, cotangent, w_value, w_radial, type_gain, w_out) + tuple(early),
        [
            pltpu.VMEM((6, 8, slots), f32),
            pltpu.VMEM((2 * outer, channels), bf16),
            pltpu.VMEM((2 * outer, channels), bf16),
            pltpu.VMEM((channels, 2 * outer), bf16),
            pltpu.VMEM((kinds, 2 * outer), bf16),
            pltpu.VMEM((channels, 2 * outer), f32),
            pltpu.VMEM((channels, 2 * outer), f32),
            pltpu.VMEM((basis_count, channels, slots), f32),
            pltpu.VMEM((channels, tall), f32),
            pltpu.VMEM((2, rows, channels), bf16),
        ]
        + [pltpu.VMEM((tall, outer), bf16)] * 2
        + [pltpu.VMEM((3, slots, outer), f32)] * 2
        + [pltpu.VMEM((channels, tall), f32)] * 2
        + [pltpu.VMEM((tall, channels), bf16)] * 2
        + [pltpu.VMEM((channels, tall), bf16)] * 2
        + [pltpu.VMEM((tall, inner), f32)] * 2
        + [pltpu.VMEM((tall, outer), f32)] * 2
        + [
            pltpu.VMEM((channels, inner), f32),
            pltpu.VMEM((channels, 2 * outer), f32),
            pltpu.VMEM((2, 3, slots, slots), f32),
            pltpu.VMEM((12, 3, 8, slots), f32),
        ],
    )
    got_b = lax.ppermute(pay_b, "gx", x_odd)
    got_a = lax.ppermute(pay_a, "gx", x_even)
    if len(x_even) == 4:
        other = lax.ppermute(keep, "gx", across("gx", 2))
        total = add(keep, got_a[:rows]) + add(other, got_b[:rows])
    else:
        total = add(keep, got_a[:rows])
        step = 2
        while step < len(x_even):
            part = total.astype(bf16)
            total = add(part, lax.ppermute(part, "gx", across("gx", step)))
            step *= 2
    part = total.astype(bf16)
    corner_b = own_acc[0] + add(got_a[rows : rows + size], got_b[rows : rows + size])
    corner_a = own_acc[3] + add(got_a[rows + size :], got_b[rows + size :])
    got = lax.ppermute(jnp.concatenate([part, corner_a.astype(bf16)]), "gy", y_even)
    far = lax.ppermute(corner_b.astype(bf16), "gy", y_odd)
    total = add(part, got[:rows])
    step = 2
    while step < len(y_even):
        part = total.astype(bf16)
        total = add(part, lax.ppermute(part, "gy", across("gy", step)))
        step *= 2
    half = lax.ppermute(total, "gx", x_even)
    fold_a, fold_b, got = lax.optimization_barrier((fold_a, fold_b, got))
    own_b = lax.ppermute(fold_b, "gx", x_odd)
    own_a = lax.ppermute(fold_a, "gx", x_even)
    grad_feat, grad_pos = call(
        cells_kernel, 4,
        (shape(features.shape, bf16), shape((row_count, 3, col_count, slots), f32)),
        (own_acc, own_a, own_b, far, got, bead_types, cotangent, w_value, type_gain),
    )
    wvalue, wradial, ggain, wout = call(
        weights_kernel, 4,
        (
            shape((channels, channels), f32),
            shape((basis_count, channels), f32),
            shape((type_count, channels), f32),
            shape((channels, channels), f32),
        ),
        (total, half),
    )
    return out_feat, grad_feat, jnp.swapaxes(grad_pos, 1, 2), wvalue, wradial, ggain, wout


def solution(mesh):
    cell = P(("frame", "gx"), "gy", None, None)

    return jax.shard_map(
        on_device,
        mesh=mesh,
        in_specs=(
            cell, cell, P(("frame", "gx"), "gy", None), P(("frame", "gx"), "gy"),
            P(), P(), P(), P(), cell,
        ),
        out_specs=(cell, cell, cell) + (P("frame", None),) * 4,
        check_vma=False,
    )
```

profile of v0, /device:TPU:0, one launch (start us, length us, event | category | flops | bytes accessed | tf_op | source)
XLA Modules:
  0.0 51.8 jit_solution(13559286293074693666)
XLA Ops:
  0.6 0.1 pad_add_fusion.order
  0.7 1.6 %pack.1 = (bf16[2,144,128]{2,1,0:T(8,128)(2,1)S(1)}, s32[1,2,128]{2,1,0:T(2,128)S(1)}, bf16[1,2,128,128]{3,2,1,0:T(8,128)(2,1)S(1)}, bf16[128,128]{1,0:T(8,128)(...) custom-call(s32[2]{0:T(128)S(1)} %pad_add_fusion.order, s32[1,2]{1,0:T(1,128)} %counts.1, ...), custom_call_target="tpu_custom_call" | custom-call | tf_op jit(solution)/shard_map/pack/pallas_call | solution.py:491
  2.3 2.5 %collective-permute-start.1 = (bf16[2,144,128]{2,1,0:T(8,128)(2,1)S(1)}, bf16[2,144,128]{2,1,0:T(8,128)(2,1)S(1)}, u32[]{:S(2)}, u32[]{:S(2)}) collective-permute-start(bf16[2,144,128]{2,1,0:T(8,128)(2,1)S(1)} %get-tuple-element.44.own), channel_id=1, source_target_pairs={{0,24},{8,16},{16,8},{24,0},{1,25},{9,17},{17,9},{25,1},{2,26},{10... | collective-permute-start | bytes 221192 | tf_op jit(solution)/shard_map/ppermute | solution.py:516
  4.8 0.7 %collective-permute-start = (bf16[2,144,128]{2,1,0:T(8,128)(2,1)S(1)}, bf16[2,144,128]{2,1,0:T(8,128)(2,1)S(1)}, u32[]{:S(2)}, u32[]{:S(2)}) collective-permute-start(bf16[2,144,128]{2,1,0:T(8,128)(2,1)S(1)} %get-tuple-element.44.own), channel_id=1, source_target_pairs={{0,8},{8,0},{16,24},{24,16},{1,9},{9,1},{17,25},{25,17},{2,10},{10... | collective-permute-start | bytes 221192 | tf_op jit(solution)/shard_map/ppermute | solution.py:517
  5.5 2.0 %collective-permute-done.1.row_b = bf16[2,144,128]{2,1,0:T(8,128)(2,1)S(1)} collective-permute-done((bf16[2,144,128]{2,1,0:T(8,128)(2,1)S(1)}, bf16[2,144,128]{2,1,0:T(8,128)(2,1)S(1)}, u32[]{:S(2)}, u32[]{:S(2)}) %collective-permute-start.1) | collective-permute-done | bytes 73760 | tf_op jit(solution)/shard_map/ppermute | solution.py:516
  7.5 0.0 collective-permute-done.row_a
  7.5 2.5 %collective-permute-start.2 = (bf16[3,144,128]{2,1,0:T(8,128)(2,1)S(1)}, bf16[3,144,128]{2,1,0:T(8,128)(2,1)S(1)}, u32[]{:S(2)}, u32[]{:S(2)}) collective-permute-start(bf16[3,144,128]{2,1,0:T(8,128)(2,1)S(1)} %pad_maximum_fusion), channel_id=1, source_target_pairs={{0,2},{2,0},{4,6},{6,4},{1,3},{3,1},{5,7},{7,5},{8,10},{10,8},{12,... | collective-permute-start | bytes 331784 | tf_op jit(solution)/shard_map/ppermute | solution.py:519
  10.1 2.5 %collective-permute-start.3 = (bf16[3,144,128]{2,1,0:T(8,128)(2,1)S(1)}, bf16[3,144,128]{2,1,0:T(8,128)(2,1)S(1)}, u32[]{:S(2)}, u32[]{:S(2)}) collective-permute-start(bf16[3,144,128]{2,1,0:T(8,128)(2,1)S(1)} %pad_maximum_fusion.1), channel_id=1, source_target_pairs={{0,6},{2,4},{4,2},{6,0},{1,7},{3,5},{5,3},{7,1},{8,14},{10,12},{12... | collective-permute-start | bytes 331784 | tf_op jit(solution)/shard_map/ppermute | solution.py:518
  12.6 4.2 %shard_map.144 = (f32[6,8,128]{2,1,0:T(8,128)S(1)}, f32[2,3,128,128]{3,2,1,0:T(8,128)S(1)}, bf16[768,128]{1,0:T(8,128)(2,1)S(1)}, bf16[768,128]{1,0:T(8,128)(2,1...) custom-call(s32[2]{0:T(128)S(1)} %pad_add_fusion.order, ...), custom_call_target="tpu_custom_call" | custom-call | tf_op jit(solution)/shard_map/pallas_call | solution.py:481
  16.8 0.0 collective-permute-done.2.col_a
  16.8 1.3 %collective-permute-done.3.col_b = bf16[3,144,128]{2,1,0:T(8,128)(2,1)S(1)} collective-permute-done((bf16[3,144,128]{2,1,0:T(8,128)(2,1)S(1)}, bf16[3,144,128]{2,1,0:T(8,128)(2,1)S(1)}, u32[]{:S(2)}, u32[]{:S(2)}) %collective-permute-start.3) | collective-permute-done | bytes 110624 | tf_op jit(solution)/shard_map/ppermute | solution.py:518
  18.0 9.0 %shard_map.145 = (bf16[1,2,128,128]{3,2,1,0:T(8,128)(2,1)}, bf16[144,128]{1,0:T(8,128)(2,1)S(1)}, bf16[432,128]{1,0:T(8,128)(2,1)S(1)}, bf16[432,128]{1,0:T(8,12...) custom-call(s32[2]{0:T(128)S(1)} %pad_add_fusion.order, ...), custom_call_target="tpu_custom_call" | custom-call | tf_op jit(solution)/shard_map/pallas_call | solution.py:481
  27.0 0.0 collective-permute-start.4
  27.0 1.7 %collective-permute-start.6 = (bf16[432,128]{1,0:T(8,128)(2,1)S(1)}, bf16[432,128]{1,0:T(8,128)(2,1)S(1)}, u32[]{:S(2)}, u32[]{:S(2)}) collective-permute-start(bf16[432,128]{1,0:T(8,128)(2,1)S(1)} %get-tuple-element.70), channel_id=1, source_target_pairs={{0,24},{8,16},{16,8},{24,0},{1,25},{9,17},{17,9},{25,1},{2,26},{10... | collective-permute-start | bytes 331784 | tf_op jit(solution)/shard_map/ppermute | solution.py:575
  28.7 0.4 collective-permute-start.5
  29.2 4.0 %collective-permute-done.5 = bf16[144,128]{1,0:T(8,128)(2,1)S(1)} collective-permute-done((bf16[144,128]{1,0:T(8,128)(2,1)S(1)}, bf16[144,128]{1,0:T(8,128)(2,1)S(1)}, u32[]{:S(2)}, u32[]{:S(2)}) %collective-permute-start.5) | collective-permute-done | bytes 36896 | tf_op jit(solution)/shard_map/ppermute | solution.py:578
  33.2 0.0 collective-permute-done.4
  33.2 0.0 collective-permute-done.6
  33.2 0.1 fusion
  33.3 0.7 %collective-permute-start.7 = (bf16[288,128]{1,0:T(8,128)(2,1)S(1)}, bf16[288,128]{1,0:T(8,128)(2,1)S(1)}, u32[]{:S(2)}, u32[]{:S(2)}) collective-permute-start(bf16[288,128]{1,0:T(8,128)(2,1)S(1)} %pad_maximum_fusion.2), channel_id=1, source_target_pairs={{0,2},{2,0},{4,6},{6,4},{1,3},{3,1},{5,7},{7,5},{8,10},{10,8},{12,... | collective-permute-start | bytes 221192 | tf_op jit(solution)/shard_map/ppermute | solution.py:590
  34.0 3.7 %collective-permute-done.7.near = bf16[288,128]{1,0:T(8,128)(2,1)S(1)} collective-permute-done((bf16[288,128]{1,0:T(8,128)(2,1)S(1)}, bf16[288,128]{1,0:T(8,128)(2,1)S(1)}, u32[]{:S(2)}, u32[]{:S(2)}) %collective-permute-start.7) | collective-permute-done | bytes 73760 | tf_op jit(solution)/shard_map/ppermute | solution.py:590
  37.7 1.9 %collective-permute-start.11 = (bf16[144,128]{1,0:T(8,128)(2,1)S(1)}, bf16[144,128]{1,0:T(8,128)(2,1)S(1)}, u32[]{:S(2)}, u32[]{:S(2)}) collective-permute-start(bf16[144,128]{1,0:T(8,128)(2,1)S(1)} %add_convert_fusion), channel_id=1, source_target_pairs={{0,4},{2,6},{4,0},{6,2},{1,5},{3,7},{5,1},{7,3},{8,12},{10,14},{12... | collective-permute-start | bytes 110600 | tf_op jit(solution)/shard_map/ppermute | solution.py:596
  39.6 0.0 collective-permute-start.8
  39.6 1.7 %collective-permute-start.9 = (bf16[288,128]{1,0:T(8,128)(2,1)S(1)}, bf16[288,128]{1,0:T(8,128)(2,1)S(1)}, u32[]{:S(2)}, u32[]{:S(2)}) collective-permute-start(bf16[288,128]{1,0:T(8,128)(2,1)S(1)} %get-tuple-element.72), channel_id=1, source_target_pairs={{0,24},{8,16},{16,8},{24,0},{1,25},{9,17},{17,9},{25,1},{2,26},{10... | collective-permute-start | bytes 221192 | tf_op jit(solution)/shard_map/ppermute | solution.py:600
  41.3 1.7 %collective-permute-done.11 = bf16[144,128]{1,0:T(8,128)(2,1)S(1)} collective-permute-done((bf16[144,128]{1,0:T(8,128)(2,1)S(1)}, bf16[144,128]{1,0:T(8,128)(2,1)S(1)}, u32[]{:S(2)}, u32[]{:S(2)}) %collective-permute-start.11) | collective-permute-done | bytes 36896 | tf_op jit(solution)/shard_map/ppermute | solution.py:596
  43.0 0.1 collective-permute-start.12
  43.1 1.2 %collective-permute-start.10 = (bf16[144,128]{1,0:T(8,128)(2,1)S(1)}, bf16[144,128]{1,0:T(8,128)(2,1)S(1)}, u32[]{:S(2)}, u32[]{:S(2)}) collective-permute-start(bf16[144,128]{1,0:T(8,128)(2,1)S(1)} %get-tuple-element.81), channel_id=1, source_target_pairs={{0,6},{2,4},{4,2},{6,0},{1,7},{3,5},{5,3},{7,1},{8,14},{10,12},{12... | collective-permute-start | bytes 110600 | tf_op jit(solution)/shard_map/ppermute | solution.py:591
  44.3 4.7 %collective-permute-done.10.far = bf16[144,128]{1,0:T(8,128)(2,1)S(1)} collective-permute-done((bf16[144,128]{1,0:T(8,128)(2,1)S(1)}, bf16[144,128]{1,0:T(8,128)(2,1)S(1)}, u32[]{:S(2)}, u32[]{:S(2)}) %collective-permute-start.10) | collective-permute-done | bytes 36896 | tf_op jit(solution)/shard_map/ppermute | solution.py:591
  48.9 0.0 collective-permute-done.8.got_a
  48.9 0.0 collective-permute-done.9.got_b
  48.9 1.6 %shard_map.146 = (bf16[1,2,128,128]{3,2,1,0:T(8,128)(2,1)}, f32[1,3,2,128]{3,2,1,0:T(2,128)}) custom-call(s32[2]{0:T(128)S(1)} %pad_add_fusion.order, f32[4,144,128]{2,1,0:T(8,128)S(1)} %get-tuple-element.65.own, bf16[288,128]{1,0:T(8,128)(2,1)S(1)} %collective-permute-done.8.got_a, bf16[288,128]{1,0:T(8,128)(2,1)S(1)} %collective-permute-done.9.got_b, ...), custom_call_target="tpu_custom_call" | custom-call | tf_op jit(solution)/shard_map/pallas_call | solution.py:481
  50.6 0.0 collective-permute-done.12.other
  50.6 1.2 %shard_map.147 = (f32[128,128]{1,0:T(8,128)}, f32[8,128]{1,0:T(8,128)}, f32[16,128]{1,0:T(8,128)}, f32[128,128]{1,0:T(8,128)}) custom-call(s32[2]{0:T(128)S(1)} %pad_add_fusion.order, f32[144,128]{1,0:T(8,128)S(1)} %convert_add_fusion.mine, f32[144,128]{1,0:T(8,128)S(1)} %collective-permute-done.12.other), custom_call_target="tpu_custom_call" | custom-call | tf_op jit(solution)/shard_map/pallas_call | solution.py:481
  (8 shorter events, 0.1 us)
Async XLA Ops:
  2.3 5.2 %collective-permute-start.1 = (bf16[2,144,128]{2,1,0:T(8,128)(2,1)S(1)}, bf16[2,144,128]{2,1,0:T(8,128)(2,1)S(1)}, u32[]{:S(2)}, u32[]{:S(2)}) collective-permute-start(bf16[2,144,128]{2,1,0:T(8,128)(2,1)S(1)} %get-tuple-element.44.own), channel_id=1, source_target_pairs={{0,24},{8,16},{16,8},{24,0},{1,25},{9,17},{17,9},{25,1},{2,26},{10... | collective-permute-start | bytes 221192 | tf_op jit(solution)/shard_map/ppermute | solution.py:516
  4.8 2.7 %collective-permute-start = (bf16[2,144,128]{2,1,0:T(8,128)(2,1)S(1)}, bf16[2,144,128]{2,1,0:T(8,128)(2,1)S(1)}, u32[]{:S(2)}, u32[]{:S(2)}) collective-permute-start(bf16[2,144,128]{2,1,0:T(8,128)(2,1)S(1)} %get-tuple-element.44.own), channel_id=1, source_target_pairs={{0,8},{8,0},{16,24},{24,16},{1,9},{9,1},{17,25},{25,17},{2,10},{10... | collective-permute-start | bytes 221192 | tf_op jit(solution)/shard_map/ppermute | solution.py:517
  7.5 9.2 %collective-permute-start.2 = (bf16[3,144,128]{2,1,0:T(8,128)(2,1)S(1)}, bf16[3,144,128]{2,1,0:T(8,128)(2,1)S(1)}, u32[]{:S(2)}, u32[]{:S(2)}) collective-permute-start(bf16[3,144,128]{2,1,0:T(8,128)(2,1)S(1)} %pad_maximum_fusion), channel_id=1, source_target_pairs={{0,2},{2,0},{4,6},{6,4},{1,3},{3,1},{5,7},{7,5},{8,10},{10,8},{12,... | collective-permute-start | bytes 331784 | tf_op jit(solution)/shard_map/ppermute | solution.py:519
  10.1 8.0 %collective-permute-start.3 = (bf16[3,144,128]{2,1,0:T(8,128)(2,1)S(1)}, bf16[3,144,128]{2,1,0:T(8,128)(2,1)S(1)}, u32[]{:S(2)}, u32[]{:S(2)}) collective-permute-start(bf16[3,144,128]{2,1,0:T(8,128)(2,1)S(1)} %pad_maximum_fusion.1), channel_id=1, source_target_pairs={{0,6},{2,4},{4,2},{6,0},{1,7},{3,5},{5,3},{7,1},{8,14},{10,12},{12... | collective-permute-start | bytes 331784 | tf_op jit(solution)/shard_map/ppermute | solution.py:518
  27.0 6.2 %collective-permute-start.4 = (bf16[432,128]{1,0:T(8,128)(2,1)S(1)}, bf16[432,128]{1,0:T(8,128)(2,1)S(1)}, u32[]{:S(2)}, u32[]{:S(2)}) collective-permute-start(bf16[432,128]{1,0:T(8,128)(2,1)S(1)} %get-tuple-element.69), channel_id=1, source_target_pairs={{0,8},{8,0},{16,24},{24,16},{1,9},{9,1},{17,25},{25,17},{2,10},{10... | collective-permute-start | bytes 331784 | tf_op jit(solution)/shard_map/ppermute | solution.py:576
  27.0 6.2 %collective-permute-start.6 = (bf16[432,128]{1,0:T(8,128)(2,1)S(1)}, bf16[432,128]{1,0:T(8,128)(2,1)S(1)}, u32[]{:S(2)}, u32[]{:S(2)}) collective-permute-start(bf16[432,128]{1,0:T(8,128)(2,1)S(1)} %get-tuple-element.70), channel_id=1, source_target_pairs={{0,24},{8,16},{16,8},{24,0},{1,25},{9,17},{17,9},{25,1},{2,26},{10... | collective-permute-start | bytes 331784 | tf_op jit(solution)/shard_map/ppermute | solution.py:575
  28.7 4.5 %collective-permute-start.5 = (bf16[144,128]{1,0:T(8,128)(2,1)S(1)}, bf16[144,128]{1,0:T(8,128)(2,1)S(1)}, u32[]{:S(2)}, u32[]{:S(2)}) collective-permute-start(bf16[144,128]{1,0:T(8,128)(2,1)S(1)} %get-tuple-element.68), channel_id=1, source_target_pairs={{0,16},{8,24},{16,0},{24,8},{1,17},{9,25},{17,1},{25,9},{2,18},{10... | collective-permute-start | bytes 110600 | tf_op jit(solution)/shard_map/ppermute | solution.py:578
  33.3 4.4 %collective-permute-start.7 = (bf16[288,128]{1,0:T(8,128)(2,1)S(1)}, bf16[288,128]{1,0:T(8,128)(2,1)S(1)}, u32[]{:S(2)}, u32[]{:S(2)}) collective-permute-start(bf16[288,128]{1,0:T(8,128)(2,1)S(1)} %pad_maximum_fusion.2), channel_id=1, source_target_pairs={{0,2},{2,0},{4,6},{6,4},{1,3},{3,1},{5,7},{7,5},{8,10},{10,8},{12,... | collective-permute-start | bytes 221192 | tf_op jit(solution)/shard_map/ppermute | solution.py:590
  37.7 5.3 %collective-permute-start.11 = (bf16[144,128]{1,0:T(8,128)(2,1)S(1)}, bf16[144,128]{1,0:T(8,128)(2,1)S(1)}, u32[]{:S(2)}, u32[]{:S(2)}) collective-permute-start(bf16[144,128]{1,0:T(8,128)(2,1)S(1)} %add_convert_fusion), channel_id=1, source_target_pairs={{0,4},{2,6},{4,0},{6,2},{1,5},{3,7},{5,1},{7,3},{8,12},{10,14},{12... | collective-permute-start | bytes 110600 | tf_op jit(solution)/shard_map/ppermute | solution.py:596
  39.6 9.3 %collective-permute-start.8 = (bf16[288,128]{1,0:T(8,128)(2,1)S(1)}, bf16[288,128]{1,0:T(8,128)(2,1)S(1)}, u32[]{:S(2)}, u32[]{:S(2)}) collective-permute-start(bf16[288,128]{1,0:T(8,128)(2,1)S(1)} %get-tuple-element.71), channel_id=1, source_target_pairs={{0,8},{8,0},{16,24},{24,16},{1,9},{9,1},{17,25},{25,17},{2,10},{10... | collective-permute-start | bytes 221192 | tf_op jit(solution)/shard_map/ppermute | solution.py:601
  39.6 9.3 %collective-permute-start.9 = (bf16[288,128]{1,0:T(8,128)(2,1)S(1)}, bf16[288,128]{1,0:T(8,128)(2,1)S(1)}, u32[]{:S(2)}, u32[]{:S(2)}) collective-permute-start(bf16[288,128]{1,0:T(8,128)(2,1)S(1)} %get-tuple-element.72), channel_id=1, source_target_pairs={{0,24},{8,16},{16,8},{24,0},{1,25},{9,17},{17,9},{25,1},{2,26},{10... | collective-permute-start | bytes 221192 | tf_op jit(solution)/shard_map/ppermute | solution.py:600
  43.0 7.5 %collective-permute-start.12 = (f32[144,128]{1,0:T(8,128)S(1)}, f32[144,128]{1,0:T(8,128)S(1)}, u32[]{:S(2)}, u32[]{:S(2)}) collective-permute-start(f32[144,128]{1,0:T(8,128)S(1)} %convert_add_fusion.mine), channel_id=1, source_target_pairs={{0,8},{8,0},{16,24},{24,16},{1,9},{9,1},{17,25},{25,17},{2,10},{10... | collective-permute-start | bytes 221192 | tf_op jit(solution)/shard_map/ppermute | solution.py:598
  43.1 5.8 %collective-permute-start.10 = (bf16[144,128]{1,0:T(8,128)(2,1)S(1)}, bf16[144,128]{1,0:T(8,128)(2,1)S(1)}, u32[]{:S(2)}, u32[]{:S(2)}) collective-permute-start(bf16[144,128]{1,0:T(8,128)(2,1)S(1)} %get-tuple-element.81), channel_id=1, source_target_pairs={{0,6},{2,4},{4,2},{6,0},{1,7},{3,5},{5,3},{7,1},{8,14},{10,12},{12... | collective-permute-start | bytes 110600 | tf_op jit(solution)/shard_map/ppermute | solution.py:591
where the time goes:
time: 51.9 us; the launch traced here: 51.8 us
  Pallas kernels  17.6 us (34%)
  waiting for transfers between devices  17.3 us (33%)
  starting transfers between devices  15.9 us (31%)
  between operations  0.73 us (1%)
    pallas_call x4, Pallas kernels, call(): pl.pallas_call(kernel, out_shape=out_shape, in_specs=[smem] + [vmem] * le...  16 us
    ppermute x1, waiting for transfers between devices, on_device(): far = lax.ppermute(corner_b.astype(bf16), 'gy', y_odd)  4.67 us
    ppermute x1, waiting for transfers between devices, on_device(): other = lax.ppermute(keep, 'gx', across('gx', 2))  4.01 us
    ppermute x1, waiting for transfers between devices, on_device(): lax.ppermute(jnp.concatenate([part, corner_a.astype(bf16)]), 'gy', y_even)  3.68 us
    ppermute x1, starting transfers between devices, on_device(): lax.ppermute(jnp.stack([row_a[0], packed[0], row_b[0]]), 'gy', y_odd)  2.54 us
    ppermute x1, starting transfers between devices, on_device(): lax.ppermute(jnp.stack([row_a[1], packed[1], row_b[1]]), 'gy', y_even)  2.52 us
    ppermute x1, starting transfers between devices, on_device(): row_b = lax.ppermute(packed, 'gx', x_odd)  2.5 us
    ppermute x1, waiting for transfers between devices, on_device(): row_b = lax.ppermute(packed, 'gx', x_odd)  1.98 us
  transfers between devices with their start and end apart: 13, of which 6 were waited for; matrix products, arithmetic and copies ran while one was open for 0% of the time, Pallas kernels for 11%

commit v1 on v0

--- a/solution.py
+++ b/solution.py
@@ -59,11 +59,11 @@
 
 def pack_kernel(
     order, counts, feat, pos, types, cotangent, w_value, w_radial, type_gain, w_out,
-    packed, types_out, cotangent_out, w_value_out, w_radial_out, type_gain_out, w_out_out,
-    counts_here, pos_here, sems,
+    packed, cotangent_out, w_value_out, w_radial_out, type_gain_out, w_out_out,
+    counts_here, pos_here, types_here, sems,
 ):
     slots = feat.shape[2]
-    moves = [(counts, counts_here), (pos, pos_here), (types, types_out)]
+    moves = [(counts, counts_here), (pos, pos_here), (types, types_here)]
     for place in range(2):
         cell = jnp.where(order[1] == 0, place, 1 - place)
         moves.append((feat.at[0, cell], packed.at[place, 0:slots, :]))
@@ -89,7 +89,7 @@
             for which, part in enumerate(split3(row)):
                 parts[which].append(part.astype(f32))
         rows = parts[0] + parts[1] + parts[2]
-        rows.append(types_out[0, pl.ds(cell, 1), :].astype(f32))
+        rows.append(types_here[0, pl.ds(cell, 1), :].astype(f32))
         rows.append(jnp.zeros((AUX - len(rows), slots), f32))
         packed[place, slots : slots + AUX, :] = jnp.concatenate(rows, axis=0).astype(bf16)
     for copy in copies[3:]:
@@ -220,13 +220,12 @@
 
 def main_kernel(
     basis_count, order, col_a, col_b, cotangent, w_value, w_radial, type_gain, w_out,
-    in_pos, own_pos, in_feat, in_val, in_carried_t, in_onehot, in_projected, in_gains,
-    in_weights_b, in_weights_a, in_terms_b, in_terms_a, in_summed_b, in_summed_a,
+    own_pos, in_feat, in_carried_t, in_onehot, in_projected, in_gains,
+    in_weights_b, in_weights_a, in_summed_b, in_summed_a,
     out_feat, keep, pay_a, pay_b, fold_a, fold_b, own_acc,
-    out_pos, ot_feat, ot_val, ot_carried_t, ot_onehot, ot_projected, ot_gains, columns, products, whole,
-    ot_weights_b, ot_weights_a, ot_terms_b, ot_terms_a, summed_b, summed_a,
-    scaled_b, scaled_a, scaled_tb, scaled_ta,
-    in_grad_b, in_grad_a, ot_grad_b, ot_grad_a, in_back, ot_back, pull_own, pull_far,
+    out_pos, ot_val, ot_terms_b, ot_terms_a, scaled_b, scaled_a,
+    ot_feat, ot_carried_t, ot_onehot, ot_projected, ot_gains, columns, products, whole,
+    ot_weights_b, ot_weights_a, summed_b, summed_a, scaled_tb, scaled_ta, in_back, ot_back,
 ):
     slots, channels = cotangent.shape[2], cotangent.shape[3]
     type_count = type_gain.shape[0]
@@ -234,10 +233,9 @@
     strips = slots // STRIP
     chunk = basis_count * slots // strips
     in_weights, ot_weights = (in_weights_b, in_weights_a), (ot_weights_b, ot_weights_a)
-    in_terms, ot_terms = (in_terms_b, in_terms_a), (ot_terms_b, ot_terms_a)
+    ot_terms = (ot_terms_b, ot_terms_a)
     in_summed, summed = (in_summed_b, in_summed_a), (summed_b, summed_a)
     scaled, scaled_t = (scaled_b, scaled_a), (scaled_tb, scaled_ta)
-    in_grad, ot_grad = (in_grad_b, in_grad_a), (ot_grad_b, ot_grad_a)
     for index in range(6):
         place, row = index // 3, index % 3
         ref = (col_b, col_a)[place]
@@ -293,64 +291,20 @@
             products[:, here] = product if place == 0 else products[:, here] + product
         return dot(aggregate_t.astype(bf16), grad_pre)
 
-    def weight_grads(place, s):
-        rows = chunk_of(s, chunk)
-        in_grad[place][rows, :] = dot_t(scaled[place][rows, :], in_val[...])
-        ot_grad[place][rows, :] = dot_t(scaled[place][rows, :], ot_val[outer(place), :])
-
-    def pulls(place, s):
-        first, strip = strip_of(s)
-        own_xyz = [own_pos[place, comp, strip, :] for comp in range(3)]
-        total = [jnp.zeros((STRIP, slots), f32) for _ in range(3)]
-        for block in range(9):
-            inner = block < 6
-            grad = (in_grad if inner else ot_grad)[place]
-            terms = (in_terms if inner else ot_terms)[place]
-            cells = in_pos if inner else out_pos
-            cell = block if inner else place * 3 + block - 6
-            index = block if inner else 6 + cell
-            local = block if inner else block - 6
-            there = slice(local * slots, (local + 1) * slots)
-
-            def grad_of(k):
-                rows = pl.ds(pl.multiple_of(first + k * slots, STRIP), STRIP)
-                return grad[rows, there]
-
-            step = terms[0, strip, there]
-            value = grad_of(basis_count - 1)
-            slope = None
-            for k in range(basis_count - 2, -1, -1):
-                slope = value if slope is None else value + step * slope
-                value = grad_of(k) + step * value
-            pull = terms[1, strip, there] * value + terms[2, strip, there] * slope
-            for comp in range(3):
-                force = pull * (cells[cell, comp : comp + 1, :] - own_xyz[comp])
-                total[comp] = total[comp] + force
-                pull_far[index, comp] += (force[0:8] + force[8:16]) + (force[16:24] + force[24:32])
-        for comp in range(3):
-            pull_own[place, comp, strip, :] = total[comp]
-
-    def value_grads(s):
-        rows = chunk_of(s, chunk)
-        parts = [scaled_t[place][:, rows] for place in range(2)]
-        in_back[...] += dot(parts[0], in_weights[0][rows, :]) + dot(parts[1], in_weights[1][rows, :])
-        for place in range(2):
-            ot_back[:, outer(place)] += dot(parts[place], ot_weights[place][rows, :])
+    def value_grads(place):
+        inner = dot(scaled_t[place][...], in_weights[place][...])
+        in_back[...] = inner if place == 0 else in_back[...] + inner
+        ot_back[:, outer(place)] = dot(scaled_t[place][...], ot_weights[place][...])
 
     run = functools.partial
-    pull_far[...] = jnp.zeros_like(pull_far)
-    in_back[...] = jnp.zeros_like(in_back)
-    ot_back[...] = jnp.zeros_like(ot_back)
     stage(strips, run(pairs, 0))
     stage(strips, run(sums, 0), run(pairs, 1))
     for s in range(strips):
         sums(1, s)
     wout = epilogue(0)
-    for s in range(strips):
-        weight_grads(0, s)
+    value_grads(0)
     wout = wout + epilogue(1)
-    stage(strips, run(weight_grads, 1), run(pulls, 0))
-    stage(strips, value_grads, run(pulls, 1))
+    value_grads(1)
 
     wvalue = ggain = None
     for back, feat, onehot, projected, gains in (
@@ -379,55 +333,108 @@
     keep[...] = whole[order[0]]
     for ref in (pay_a, pay_b):
         ref[0:rows, :] = whole[1 - order[0]]
-    force = float(basis_count - 1)
-    size = slots + AUX
     for col in range(4):
         for row in range(3):
             inner = col in (1, 2)
             local = (col - 1) * 3 + row if inner else (0 if col == 0 else 3) + row
             back = (in_back if inner else ot_back)[:, local * slots : (local + 1) * slots]
-            lines = []
+            if row == 1:
+                own_acc[col] = back
+            elif inner:
+                ref = fold_a if row == 0 else fold_b
+                ref[(col - 1) * slots : col * slots, :] = back.astype(bf16)
+            else:
+                ref = pay_a if row == 0 else pay_b
+                base = rows + (0 if col == 0 else slots)
+                ref[base : base + slots, :] = back.astype(bf16)
+
+
+def pulls_kernel(
+    basis_count, order, in_pos, own_pos, in_val, in_terms_b, in_terms_a, out_pos, ot_val,
+    ot_terms_b, ot_terms_a, scaled_b, scaled_a,
+    lines,
+    in_grad_b, in_grad_a, ot_grad_b, ot_grad_a, pull_own, pull_far,
+):
+    slots = in_pos.shape[2]
+    third = 3 * slots
+    strips = slots // STRIP
+    chunk = basis_count * slots // strips
+    in_terms, ot_terms = (in_terms_b, in_terms_a), (ot_terms_b, ot_terms_a)
+    scaled = (scaled_b, scaled_a)
+    in_grad, ot_grad = (in_grad_b, in_grad_a), (ot_grad_b, ot_grad_a)
+
+    def weight_grads(place, s):
+        rows = chunk_of(s, chunk)
+        in_grad[place][rows, :] = dot_t(scaled[place][rows, :], in_val[...])
+        outer = slice(place * third, (place + 1) * third)
+        ot_grad[place][rows, :] = dot_t(scaled[place][rows, :], ot_val[outer, :])
+
+    def pulls(place, s):
+        first, strip = strip_of(s)
+        own_xyz = [own_pos[place, comp, strip, :] for comp in range(3)]
+        total = [jnp.zeros((STRIP, slots), f32) for _ in range(3)]
+        for block in range(9):
+            inner = block < 6
+            grad = (in_grad if inner else ot_grad)[place]
+            terms = (in_terms if inner else ot_terms)[place]
+            cells = in_pos if inner else out_pos
+            cell = block if inner else place * 3 + block - 6
+            index = block if inner else 6 + cell
+            local = block if inner else block - 6
+            there = slice(local * slots, (local + 1) * slots)
+
+            def grad_of(k):
+                rows = pl.ds(pl.multiple_of(first + k * slots, STRIP), STRIP)
+                return grad[rows, there]
+
+            step = terms[0, strip, there]
+            value = grad_of(basis_count - 1)
+            slope = None
+            for k in range(basis_count - 2, -1, -1):
+                slope = value if slope is None else value + step * slope
+                value = grad_of(k) + step * value
+            pull = terms[1, strip, there] * value + terms[2, strip, there] * slope
             for comp in range(3):
-                line = jnp.sum(pull_far[local if inner else 6 + local, comp], axis=0, keepdims=True)
+                force = pull * (cells[cell, comp : comp + 1, :] - own_xyz[comp])
+                total[comp] = total[comp] + force
+                pull_far[index, comp] += (force[0:8] + force[8:16]) + (force[16:24] + force[24:32])
+        for comp in range(3):
+            pull_own[place, comp, strip, :] = total[comp]
+
+    run = functools.partial
+    pull_far[...] = jnp.zeros_like(pull_far)
+    for s in range(strips):
+        weight_grads(0, s)
+    stage(strips, run(weight_grads, 1), run(pulls, 0))
+    stage(strips, run(pulls, 1))
+    force = float(basis_count - 1)
+    rows = []
+    for col in range(4):
+        for row in range(3):
+            inner = col in (1, 2)
+            local = (col - 1) * 3 + row if inner else 6 + (0 if col == 0 else 3) + row
+            for comp in range(3):
+                line = jnp.sum(pull_far[local, comp], axis=0, keepdims=True)
                 if row == 1 and inner:
                     line = line - jnp.sum(pull_own[col - 1, comp].T, axis=0, keepdims=True)
-                lines.append(line * (force * HZ if comp == 2 else force))
-            lines.append(jnp.zeros((AUX - 3, slots), f32))
-            lines = jnp.concatenate(lines, axis=0)
-            if row == 1:
-                own_acc[col, 0:slots, :] = back
-                own_acc[col, slots:size, :] = lines
-                continue
-            if inner:
-                ref, base = (fold_a if row == 0 else fold_b), (col - 1) * size
-            else:
-                ref, base = (pay_a if row == 0 else pay_b), rows + (0 if col == 0 else size)
-            ref[base : base + slots, :] = back.astype(bf16)
-            ref[base + slots : base + size, :] = lines.astype(bf16)
-
-
-def cell_grads(own, got_a, got_b, got, types_row, cotangent, w_value, type_gain):
-    slots = cotangent.shape[0]
-    total = own + (got_a.astype(f32) + got_b.astype(f32)) + got.astype(f32)
-    gain = dot(gain_columns(type_gain), onehot_rows(types_row, type_gain.shape[0], slots))
-    half = (total[0:slots] * gain).astype(bf16)
-    feat = (cotangent.astype(f32) + dot(w_value[...], half).T).astype(bf16)
-    return feat, total[slots : slots + 3]
+                rows.append(line * (force * HZ if comp == 2 else force))
+            rows.append(jnp.zeros((1, slots), f32))
+        rows.append(jnp.zeros((4, slots), f32))
+    lines[...] = jnp.concatenate(rows, axis=0)
 
 
 def cells_kernel(
-    order, own, got_a, got_b, far, near, types, cotangent, w_value, type_gain, grad_feat, grad_pos
+    order, own, got_a, got_b, far, near, lines, cotangent, w_value, gains, grad_feat, grad_pos
 ):
-    size = far.shape[0]
+    slots = own.shape[2]
     for place in range(2):
         cell = jnp.where(order[1] == 0, place, 1 - place)
-        here = slice(place * size, (place + 1) * size)
-        got = far[...] if place == 0 else near[near.shape[0] - size :, :]
-        feat, pos = cell_grads(
-            own[place + 1], got_a[here, :], got_b[here, :], got, types[0, pl.ds(cell, 1), :],
-            cotangent[0, cell], w_value, type_gain,
-        )
-        grad_feat[0, cell] = feat
+        here = slice(place * slots, (place + 1) * slots)
+        got = far[0:slots, :] if place == 0 else near[near.shape[0] - AUX - slots : near.shape[0] - AUX, :]
+        total = own[place + 1] + add(got_a[here, :], got_b[here, :]) + got.astype(f32)
+        half = (total * gains[:, (3 * place + 1) * slots : (3 * place + 2) * slots]).astype(bf16)
+        grad_feat[0, cell] = (cotangent[0, cell].astype(f32) + dot(w_value[...], half).T).astype(bf16)
+        pos = lines[4 * place : 4 * place + 4, :]
         for comp in range(3):
             grad_pos[0, comp, pl.ds(cell, 1), :] = pos[comp : comp + 1]
 
@@ -488,17 +495,18 @@
         )(order, *arrays)
 
     hbm = pl.BlockSpec(memory_space=pltpu.HBM)
-    packed, bead_types, cotangent, w_value, w_radial, type_gain, w_out = pl.pallas_call(
+    packed, *inputs = pl.pallas_call(
         pack_kernel,
         out_shape=(
             shape((2, size, channels), bf16),
-            *(shape(a.shape, a.dtype) for a in (bead_types, cotangent, w_value, w_radial, type_gain, w_out)),
+            *(shape(a.shape, a.dtype) for a in (cotangent, w_value, w_radial, type_gain, w_out)),
         ),
         in_specs=[smem] + [hbm] * 9,
-        out_specs=(vmem,) * 7,
+        out_specs=(vmem,) * 6,
         scratch_shapes=[
             pltpu.SMEM(cell_counts.shape, jnp.int32),
             pltpu.VMEM((row_count, 3, col_count, slots), f32),
+            pltpu.VMEM(bead_types.shape, jnp.int32),
             pltpu.SemaphoreType.DMA((10,)),
         ],
         compiler_params=pltpu.CompilerParams(vmem_limit_bytes=4 * 2**20),
@@ -513,6 +521,7 @@
             )
         ),
     )
+    cotangent, w_value, w_radial, type_gain, w_out = inputs
     row_b = lax.ppermute(packed, "gx", x_odd)
     row_a = lax.ppermute(packed, "gx", x_even)
     col_b = lax.ppermute(jnp.stack([row_a[0], packed[0], row_b[0]]), "gy", y_odd)
@@ -534,21 +543,34 @@
         + (shape((channels, tall), f32),) * 2,
         (packed, row_a, row_b, w_value, type_gain),
     )
-    out_feat, keep, pay_a, pay_b, fold_a, fold_b, own_acc = call(
-        functools.partial(main_kernel, basis_count), 28,
+    (
+        in_pos, own_pos, in_feat, in_val, in_carried_t, in_onehot, in_projected, in_gains,
+        in_weights_b, in_weights_a, in_terms_b, in_terms_a, in_summed_b, in_summed_a,
+    ) = early
+    (
+        out_feat, keep, pay_a, pay_b, fold_a, fold_b, own_acc,
+        out_pos, ot_val, ot_terms_b, ot_terms_a, scaled_b, scaled_a,
+    ) = call(
+        functools.partial(main_kernel, basis_count), 16,
         (
             shape(features.shape, bf16),
             shape((rows, channels), bf16),
-            shape((rows + 2 * size, channels), bf16),
-            shape((rows + 2 * size, channels), bf16),
-            shape((2 * size, channels), bf16),
-            shape((2 * size, channels), bf16),
-            shape((4, size, slots), f32),
+            shape((rows + 2 * channels, slots), bf16),
+            shape((rows + 2 * channels, slots), bf16),
+            shape((2 * channels, slots), bf16),
+            shape((2 * channels, slots), bf16),
+            shape((4, channels, slots), f32),
+            shape((6, 8, slots), f32),
+            shape((2 * outer, channels), bf16),
+        )
+        + (shape((3, slots, outer), f32),) * 2
+        + (shape((tall, channels), bf16),) * 2,
+        (
+            col_a, col_b, cotangent, w_value, w_radial, type_gain, w_out,
+            own_pos, in_feat, in_carried_t, in_onehot, in_projected, in_gains,
+            in_weights_b, in_weights_a, in_summed_b, in_summed_a,
         ),
-        (col_a, col_b, cotangent, w_value, w_radial, type_gain, w_out) + tuple(early),
         [
-            pltpu.VMEM((6, 8, slots), f32),
-            pltpu.VMEM((2 * outer, channels), bf16),
             pltpu.VMEM((2 * outer, channels), bf16),
             pltpu.VMEM((channels, 2 * outer), bf16),
             pltpu.VMEM((kinds, 2 * outer), bf16),
@@ -559,18 +581,9 @@
             pltpu.VMEM((2, rows, channels), bf16),
         ]
         + [pltpu.VMEM((tall, outer), bf16)] * 2
-        + [pltpu.VMEM((3, slots, outer), f32)] * 2
         + [pltpu.VMEM((channels, tall), f32)] * 2
-        + [pltpu.VMEM((tall, channels), bf16)] * 2
         + [pltpu.VMEM((channels, tall), bf16)] * 2
-        + [pltpu.VMEM((tall, inner), f32)] * 2
-        + [pltpu.VMEM((tall, outer), f32)] * 2
-        + [
-            pltpu.VMEM((channels, inner), f32),
-            pltpu.VMEM((channels, 2 * outer), f32),
-            pltpu.VMEM((2, 3, slots, slots), f32),
-            pltpu.VMEM((12, 3, 8, slots), f32),
-        ],
+        + [pltpu.VMEM((channels, inner), f32), pltpu.VMEM((channels, 2 * outer), f32)],
     )
     got_b = lax.ppermute(pay_b, "gx", x_odd)
     got_a = lax.ppermute(pay_a, "gx", x_even)
@@ -584,25 +597,51 @@
             part = total.astype(bf16)
             total = add(part, lax.ppermute(part, "gx", across("gx", step)))
             step *= 2
+    lines = call(
+        functools.partial(pulls_kernel, basis_count), 20, shape((4 * AUX, slots), f32),
+        (
+            in_pos, own_pos, in_val, in_terms_b, in_terms_a, out_pos, ot_val,
+            ot_terms_b, ot_terms_a, scaled_b, scaled_a,
+        ),
+        [pltpu.VMEM((tall, inner), f32)] * 2
+        + [pltpu.VMEM((tall, outer), f32)] * 2
+        + [pltpu.VMEM((2, 3, slots, slots), f32), pltpu.VMEM((12, 3, 8, slots), f32)],
+    )
     part = total.astype(bf16)
-    corner_b = own_acc[0] + add(got_a[rows : rows + size], got_b[rows : rows + size])
-    corner_a = own_acc[3] + add(got_a[rows + size :], got_b[rows + size :])
-    got = lax.ppermute(jnp.concatenate([part, corner_a.astype(bf16)]), "gy", y_even)
-    far = lax.ppermute(corner_b.astype(bf16), "gy", y_odd)
+    corner_b = own_acc[0] + add(got_a[rows : rows + channels], got_b[rows : rows + channels])
+    corner_a = own_acc[3] + add(got_a[rows + channels :], got_b[rows + channels :])
+    sent = lines.astype(bf16)
+    got = lax.ppermute(
+        jnp.concatenate([part, corner_a.astype(bf16), sent[3 * AUX :]]), "gy", y_even
+    )
+    far = lax.ppermute(jnp.concatenate([corner_b.astype(bf16), sent[:AUX]]), "gy", y_odd)
+    lines_here = lines[AUX : 3 * AUX]
+    sent = lines_here.astype(bf16)
+    own_b = lax.ppermute(jnp.concatenate([fold_b, sent]), "gx", x_odd)
+    own_a = lax.ppermute(jnp.concatenate([fold_a, sent]), "gx", x_even)
     total = add(part, got[:rows])
     step = 2
     while step < len(y_even):
         part = total.astype(bf16)
         total = add(part, lax.ppermute(part, "gy", across("gy", step)))
         step *= 2
+    sent = jnp.concatenate([far[channels:], got[rows + channels :]])
+    more_b = lax.ppermute(sent, "gx", x_odd)
+    more_a = lax.ppermute(sent, "gx", x_even)
+    back_a = add(own_a[2 * channels :], more_a)
+    back_b = add(own_b[2 * channels :], more_b)
+    lines_here = lines_here + sent.astype(f32)
+    pos = jnp.concatenate(
+        [
+            lines_here[base + 4 : base + 8] + (back_a[base : base + 4] + back_b[base + 8 : base + 12])
+            for base in (0, AUX)
+        ]
+    )
     half = lax.ppermute(total, "gx", x_even)
-    fold_a, fold_b, got = lax.optimization_barrier((fold_a, fold_b, got))
-    own_b = lax.ppermute(fold_b, "gx", x_odd)
-    own_a = lax.ppermute(fold_a, "gx", x_even)
     grad_feat, grad_pos = call(
         cells_kernel, 4,
         (shape(features.shape, bf16), shape((row_count, 3, col_count, slots), f32)),
-        (own_acc, own_a, own_b, far, got, bead_types, cotangent, w_value, type_gain),
+        (own_acc, own_a, own_b, far, got, pos, cotangent, w_value, in_gains),
     )
     wvalue, wradial, ggain, wout = call(
         weights_kernel, 4,

time: 51.9 us -> 48.3 us (0.931)
  waiting for transfers between devices: 17.3 us -> 12.5 us
  starting transfers between devices: 15.9 us -> 17.6 us
  Pallas kernels: 17.6 us -> 17 us
    ppermute x4 -> x6, waiting for transfers between devices: 8.36 us -> 3.1 us  [the longest x1 1.95 us: on_device(): lax.ppermute(jnp.concatenate([corner_b.astype(bf16), sent[:AUX]]), 'gy',...]
    ppermute x1, waiting for transfers between devices: 4.01 us -> 0.01 us  [on_device(): other = lax.ppermute(keep, 'gx', across('gx', 2))]
    ppermute x1, waiting for transfers between devices: 0.01 us -> 2.61 us  [on_device(): got_b = lax.ppermute(pay_b, 'gx', x_odd)]
    ppermute x4 -> x6, starting transfers between devices: 3.59 us -> 5.96 us  [the longest x1 1.69 us: on_device(): more_b = lax.ppermute(sent, 'gx', x_odd)]
    ppermute x1, waiting for transfers between devices: 1.7 us -> 3.47 us  [on_device(): total = add(part, lax.ppermute(part, 'gy', across('gy', step)))]
    ppermute x1, starting transfers between devices: 1.91 us -> 1.11 us  [on_device(): total = add(part, lax.ppermute(part, 'gy', across('gy', step)))]
    pallas_call x4 -> x5, Pallas kernels: 16 us -> 15.4 us  [call(): pl.pallas_call(kernel, out_shape=out_shape, in_specs=[smem] + [vmem] * le...]
  transfers between devices with their start and end apart: 13 -> 15, of which waited for: 6 -> 7; matrix products, arithmetic and copies ran while one was open for 0% -> 0% of each run, Pallas kernels for 11% -> 12%
where the time goes in v1:
time: 48.3 us; the launch traced here: 48.1 us
  starting transfers between devices  17.6 us (36%)
  Pallas kernels  17 us (35%)
  waiting for transfers between devices  12.5 us (26%)
  between operations  0.8 us (2%)
    pallas_call x5, Pallas kernels, call(): pl.pallas_call(kernel, out_shape=out_shape, in_specs=[smem] + [vmem] * le...  15.4 us
    ppermute x1, waiting for transfers between devices, on_device(): total = add(part, lax.ppermute(part, 'gy', across('gy', step)))  3.47 us
    ppermute x1, waiting for transfers between devices, on_device(): got_b = lax.ppermute(pay_b, 'gx', x_odd)  2.61 us
    ppermute x1, starting transfers between devices, on_device(): lax.ppermute(jnp.stack([row_a[0], packed[0], row_b[0]]), 'gy', y_odd)  2.54 us
    ppermute x1, starting transfers between devices, on_device(): lax.ppermute(jnp.stack([row_a[1], packed[1], row_b[1]]), 'gy', y_even)  2.52 us
    ppermute x1, starting transfers between devices, on_device(): row_b = lax.ppermute(packed, 'gx', x_odd)  2.5 us
    ppermute x1, waiting for transfers between devices, on_device(): row_b = lax.ppermute(packed, 'gx', x_odd)  1.98 us
    ppermute x1, waiting for transfers between devices, on_device(): lax.ppermute(jnp.concatenate([corner_b.astype(bf16), sent[:AUX]]), 'gy',...  1.95 us
  transfers between devices with their start and end apart: 15, of which 7 were waited for; matrix products, arithmetic and copies ran while one was open for 0% of the time, Pallas kernels for 12%

profile of v1, /device:TPU:0, one launch (start us, length us, event | category | flops | bytes accessed | tf_op | source)
XLA Modules:
  0.0 48.1 jit_solution(72259651040598183)
XLA Ops:
  0.6 0.1 pad_add_fusion.order
  0.7 1.6 %pack.1 = (bf16[2,144,128]{2,1,0:T(8,128)(2,1)S(1)}, bf16[1,2,128,128]{3,2,1,0:T(8,128)(2,1)S(1)}, bf16[128,128]{1,0:T(8,128)(2,1)S(1)}, f32[8,128]{1,0:T(8,128)...) custom-call(s32[2]{0:T(128)S(1)} %pad_add_fusion.order, s32[1,2]{1,0:T(1,128)} %counts.1, ...), custom_call_target="tpu_custom_call" | custom-call | tf_op jit(solution)/shard_map/pack/pallas_call | solution.py:498
  2.3 2.5 %collective-permute-start.1 = (bf16[2,144,128]{2,1,0:T(8,128)(2,1)S(1)}, bf16[2,144,128]{2,1,0:T(8,128)(2,1)S(1)}, u32[]{:S(2)}, u32[]{:S(2)}) collective-permute-start(bf16[2,144,128]{2,1,0:T(8,128)(2,1)S(1)} %get-tuple-element.46.own), channel_id=1, source_target_pairs={{0,24},{8,16},{16,8},{24,0},{1,25},{9,17},{17,9},{25,1},{2,26},{10... | collective-permute-start | bytes 221192 | tf_op jit(solution)/shard_map/ppermute | solution.py:525
  4.8 0.7 %collective-permute-start = (bf16[2,144,128]{2,1,0:T(8,128)(2,1)S(1)}, bf16[2,144,128]{2,1,0:T(8,128)(2,1)S(1)}, u32[]{:S(2)}, u32[]{:S(2)}) collective-permute-start(bf16[2,144,128]{2,1,0:T(8,128)(2,1)S(1)} %get-tuple-element.46.own), channel_id=1, source_target_pairs={{0,8},{8,0},{16,24},{24,16},{1,9},{9,1},{17,25},{25,17},{2,10},{10... | collective-permute-start | bytes 221192 | tf_op jit(solution)/shard_map/ppermute | solution.py:526
  5.5 2.0 %collective-permute-done.1.row_b = bf16[2,144,128]{2,1,0:T(8,128)(2,1)S(1)} collective-permute-done((bf16[2,144,128]{2,1,0:T(8,128)(2,1)S(1)}, bf16[2,144,128]{2,1,0:T(8,128)(2,1)S(1)}, u32[]{:S(2)}, u32[]{:S(2)}) %collective-permute-start.1) | collective-permute-done | bytes 73760 | tf_op jit(solution)/shard_map/ppermute | solution.py:525
  7.5 0.0 collective-permute-done.row_a
  7.5 2.5 %collective-permute-start.2 = (bf16[3,144,128]{2,1,0:T(8,128)(2,1)S(1)}, bf16[3,144,128]{2,1,0:T(8,128)(2,1)S(1)}, u32[]{:S(2)}, u32[]{:S(2)}) collective-permute-start(bf16[3,144,128]{2,1,0:T(8,128)(2,1)S(1)} %pad_maximum_fusion), channel_id=1, source_target_pairs={{0,2},{2,0},{4,6},{6,4},{1,3},{3,1},{5,7},{7,5},{8,10},{10,8},{12,... | collective-permute-start | bytes 331784 | tf_op jit(solution)/shard_map/ppermute | solution.py:528
  10.1 2.5 %collective-permute-start.3 = (bf16[3,144,128]{2,1,0:T(8,128)(2,1)S(1)}, bf16[3,144,128]{2,1,0:T(8,128)(2,1)S(1)}, u32[]{:S(2)}, u32[]{:S(2)}) collective-permute-start(bf16[3,144,128]{2,1,0:T(8,128)(2,1)S(1)} %pad_maximum_fusion.1), channel_id=1, source_target_pairs={{0,6},{2,4},{4,2},{6,0},{1,7},{3,5},{5,3},{7,1},{8,14},{10,12},{12... | collective-permute-start | bytes 331784 | tf_op jit(solution)/shard_map/ppermute | solution.py:527
  12.6 4.1 %shard_map.144 = (f32[6,8,128]{2,1,0:T(8,128)S(1)}, f32[2,3,128,128]{3,2,1,0:T(8,128)S(1)}, bf16[768,128]{1,0:T(8,128)(2,1)S(1)}, bf16[768,128]{1,0:T(8,128)(2,1...) custom-call(s32[2]{0:T(128)S(1)} %pad_add_fusion.order, ...), custom_call_target="tpu_custom_call" | custom-call | tf_op jit(solution)/shard_map/pallas_call | solution.py:488
  16.7 0.0 collective-permute-done.2.col_a
  16.7 1.3 %collective-permute-done.3.col_b = bf16[3,144,128]{2,1,0:T(8,128)(2,1)S(1)} collective-permute-done((bf16[3,144,128]{2,1,0:T(8,128)(2,1)S(1)}, bf16[3,144,128]{2,1,0:T(8,128)(2,1)S(1)}, u32[]{:S(2)}, u32[]{:S(2)}) %collective-permute-start.3) | collective-permute-done | bytes 110624 | tf_op jit(solution)/shard_map/ppermute | solution.py:527
  18.0 4.8 %shard_map.145 = (bf16[1,2,128,128]{3,2,1,0:T(8,128)(2,1)}, bf16[144,128]{1,0:T(8,128)(2,1)S(1)}, bf16[400,128]{1,0:T(8,128)(2,1)S(1)}, bf16[400,128]{1,0:T(8,12...) custom-call(s32[2]{0:T(128)S(1)} %pad_add_fusion.order, ...), custom_call_target="tpu_custom_call" | custom-call | tf_op jit(solution)/shard_map/pallas_call | solution.py:488
  22.9 3.8 %shard_map.146 = f32[64,128]{1,0:T(8,128)S(1)} custom-call(s32[2]{0:T(128)S(1)} %pad_add_fusion.order, f32[6,8,128]{2,1,0:T(8,128)S(1)} %get-tuple-element.65.in_pos, f32[2,3,128,128]{3,2,1,0:T(8,128)S(1)} %get-tuple-element.52.own_pos, bf16[768,128]{1,0:T(8,128)(2,1)S(1)} %get-tuple-element.66.in_val, f32[3,128,768]{2,1,0:T(8,128)S(1)} %get-tuple-element.67.in_terms_b, ...), custom_call_target="tpu_custom_call" | custom-call | tf_op jit(solution)/shard_map/pallas_call | solution.py:488
  26.7 0.1 collective-permute-start.6
  26.8 1.7 %collective-permute-start.7 = (bf16[400,128]{1,0:T(8,128)(2,1)S(1)}, bf16[400,128]{1,0:T(8,128)(2,1)S(1)}, u32[]{:S(2)}, u32[]{:S(2)}) collective-permute-start(bf16[400,128]{1,0:T(8,128)(2,1)S(1)} %get-tuple-element.77), channel_id=1, source_target_pairs={{0,24},{8,16},{16,8},{24,0},{1,25},{9,17},{17,9},{25,1},{2,26},{10... | collective-permute-start | bytes 307208 | tf_op jit(solution)/shard_map/ppermute | solution.py:588
  28.5 0.4 collective-permute-start.9
  28.9 0.0 collective-permute-done.6
  28.9 2.6 %collective-permute-done.7 = bf16[400,128]{1,0:T(8,128)(2,1)S(1)} collective-permute-done((bf16[400,128]{1,0:T(8,128)(2,1)S(1)}, bf16[400,128]{1,0:T(8,128)(2,1)S(1)}, u32[]{:S(2)}, u32[]{:S(2)}) %collective-permute-start.7) | collective-permute-done | bytes 102432 | tf_op jit(solution)/shard_map/ppermute | solution.py:588
  31.6 1.5 %collective-permute-start.8 = (bf16[144,128]{1,0:T(8,128)(2,1)S(1)}, bf16[144,128]{1,0:T(8,128)(2,1)S(1)}, u32[]{:S(2)}, u32[]{:S(2)}) collective-permute-start(bf16[144,128]{1,0:T(8,128)(2,1)S(1)} %pad_maximum_fusion.5), channel_id=1, source_target_pairs={{0,6},{2,4},{4,2},{6,0},{1,7},{3,5},{5,3},{7,1},{8,14},{10,12},{12... | collective-permute-start | bytes 110600 | tf_op jit(solution)/shard_map/ppermute | solution.py:617
  33.1 0.0 collective-permute-done.9
  33.2 1.0 %collective-permute-start.10 = (bf16[288,128]{1,0:T(8,128)(2,1)S(1)}, bf16[288,128]{1,0:T(8,128)(2,1)S(1)}, u32[]{:S(2)}, u32[]{:S(2)}) collective-permute-start(bf16[288,128]{1,0:T(8,128)(2,1)S(1)} %pad_maximum_fusion.4), channel_id=1, source_target_pairs={{0,2},{2,0},{4,6},{6,4},{1,3},{3,1},{5,7},{7,5},{8,10},{10,8},{12,... | collective-permute-start | bytes 221192 | tf_op jit(solution)/shard_map/ppermute | solution.py:614
  34.2 1.4 %collective-permute-start.5 = (bf16[288,128]{1,0:T(8,128)(2,1)S(1)}, bf16[288,128]{1,0:T(8,128)(2,1)S(1)}, u32[]{:S(2)}, u32[]{:S(2)}) collective-permute-start(bf16[288,128]{1,0:T(8,128)(2,1)S(1)} %get-tuple-element.97), channel_id=1, source_target_pairs={{0,24},{8,16},{16,8},{24,0},{1,25},{9,17},{17,9},{25,1},{2,26},{10... | collective-permute-start | bytes 221192 | tf_op jit(solution)/shard_map/ppermute | solution.py:620
  35.6 0.2 collective-permute-start.4
  35.9 1.9 %collective-permute-done.8.far = bf16[144,128]{1,0:T(8,128)(2,1)S(1)} collective-permute-done((bf16[144,128]{1,0:T(8,128)(2,1)S(1)}, bf16[144,128]{1,0:T(8,128)(2,1)S(1)}, u32[]{:S(2)}, u32[]{:S(2)}) %collective-permute-start.8) | collective-permute-done | bytes 36896 | tf_op jit(solution)/shard_map/ppermute | solution.py:617
  37.8 0.8 %collective-permute-done.10.near = bf16[288,128]{1,0:T(8,128)(2,1)S(1)} collective-permute-done((bf16[288,128]{1,0:T(8,128)(2,1)S(1)}, bf16[288,128]{1,0:T(8,128)(2,1)S(1)}, u32[]{:S(2)}, u32[]{:S(2)}) %collective-permute-start.10) | collective-permute-done | bytes 73760 | tf_op jit(solution)/shard_map/ppermute | solution.py:614
  38.7 0.1 collective-permute-start.11
  38.8 1.7 %collective-permute-start.12 = (bf16[32,128]{1,0:T(8,128)(2,1)S(1)}, bf16[32,128]{1,0:T(8,128)(2,1)S(1)}, u32[]{:S(2)}, u32[]{:S(2)}) collective-permute-start(bf16[32,128]{1,0:T(8,128)(2,1)S(1)} %pad_maximum_fusion.6), channel_id=1, source_target_pairs={{0,24},{8,16},{16,8},{24,0},{1,25},{9,17},{17,9},{25,1},{2,26},{10... | collective-permute-start | bytes 24584 | tf_op jit(solution)/shard_map/ppermute | solution.py:629
  40.5 1.1 %collective-permute-start.13 = (bf16[144,128]{1,0:T(8,128)(2,1)S(1)}, bf16[144,128]{1,0:T(8,128)(2,1)S(1)}, u32[]{:S(2)}, u32[]{:S(2)}) collective-permute-start(bf16[144,128]{1,0:T(8,128)(2,1)S(1)} %add_convert_fusion), channel_id=1, source_target_pairs={{0,4},{2,6},{4,0},{6,2},{1,5},{3,7},{5,1},{7,3},{8,12},{10,14},{12... | collective-permute-start | bytes 110600 | tf_op jit(solution)/shard_map/ppermute | solution.py:626
  41.6 0.0 collective-permute-done.4.got_a
  41.6 0.0 collective-permute-done.11
  41.6 0.0 collective-permute-done.5.got_b
  41.6 0.3 collective-permute-done.12
  41.9 3.5 %collective-permute-done.13 = bf16[144,128]{1,0:T(8,128)(2,1)S(1)} collective-permute-done((bf16[144,128]{1,0:T(8,128)(2,1)S(1)}, bf16[144,128]{1,0:T(8,128)(2,1)S(1)}, u32[]{:S(2)}, u32[]{:S(2)}) %collective-permute-start.13) | collective-permute-done | bytes 36896 | tf_op jit(solution)/shard_map/ppermute | solution.py:626
  45.4 0.1 collective-permute-start.14
  45.5 1.4 %shard_map.147 = (bf16[1,2,128,128]{3,2,1,0:T(8,128)(2,1)}, f32[1,3,2,128]{3,2,1,0:T(2,128)}) custom-call(s32[2]{0:T(128)S(1)} %pad_add_fusion.order, f32[4,128,128]{2,1,0:T(8,128)S(1)} %get-tuple-element.63.own, bf16[288,128]{1,0:T(8,128)(2,1)S(1)} %collective-permute-done.4.got_a, bf16[288,128]{1,0:T(8,128)(2,1)S(1)} %collective-permute-done.5.got_b, ...), custom_call_target="tpu_custom_call" | custom-call | tf_op jit(solution)/shard_map/pallas_call | solution.py:488
  46.9 0.0 collective-permute-done.14.other
  46.9 1.2 %shard_map.148 = (f32[128,128]{1,0:T(8,128)}, f32[8,128]{1,0:T(8,128)}, f32[16,128]{1,0:T(8,128)}, f32[128,128]{1,0:T(8,128)}) custom-call(s32[2]{0:T(128)S(1)} %pad_add_fusion.order, f32[144,128]{1,0:T(8,128)S(1)} %convert_add_fusion.mine, f32[144,128]{1,0:T(8,128)S(1)} %collective-permute-done.14.other), custom_call_target="tpu_custom_call" | custom-call | tf_op jit(solution)/shard_map/pallas_call | solution.py:488
  (23 shorter events, 0.2 us)
Async XLA Ops:
  2.3 5.2 %collective-permute-start.1 = (bf16[2,144,128]{2,1,0:T(8,128)(2,1)S(1)}, bf16[2,144,128]{2,1,0:T(8,128)(2,1)S(1)}, u32[]{:S(2)}, u32[]{:S(2)}) collective-permute-start(bf16[2,144,128]{2,1,0:T(8,128)(2,1)S(1)} %get-tuple-element.46.own), channel_id=1, source_target_pairs={{0,24},{8,16},{16,8},{24,0},{1,25},{9,17},{17,9},{25,1},{2,26},{10... | collective-permute-start | bytes 221192 | tf_op jit(solution)/shard_map/ppermute | solution.py:525
  4.8 2.7 %collective-permute-start = (bf16[2,144,128]{2,1,0:T(8,128)(2,1)S(1)}, bf16[2,144,128]{2,1,0:T(8,128)(2,1)S(1)}, u32[]{:S(2)}, u32[]{:S(2)}) collective-permute-start(bf16[2,144,128]{2,1,0:T(8,128)(2,1)S(1)} %get-tuple-element.46.own), channel_id=1, source_target_pairs={{0,8},{8,0},{16,24},{24,16},{1,9},{9,1},{17,25},{25,17},{2,10},{10... | collective-permute-start | bytes 221192 | tf_op jit(solution)/shard_map/ppermute | solution.py:526
  7.5 9.2 %collective-permute-start.2 = (bf16[3,144,128]{2,1,0:T(8,128)(2,1)S(1)}, bf16[3,144,128]{2,1,0:T(8,128)(2,1)S(1)}, u32[]{:S(2)}, u32[]{:S(2)}) collective-permute-start(bf16[3,144,128]{2,1,0:T(8,128)(2,1)S(1)} %pad_maximum_fusion), channel_id=1, source_target_pairs={{0,2},{2,0},{4,6},{6,4},{1,3},{3,1},{5,7},{7,5},{8,10},{10,8},{12,... | collective-permute-start | bytes 331784 | tf_op jit(solution)/shard_map/ppermute | solution.py:528
  10.1 8.0 %collective-permute-start.3 = (bf16[3,144,128]{2,1,0:T(8,128)(2,1)S(1)}, bf16[3,144,128]{2,1,0:T(8,128)(2,1)S(1)}, u32[]{:S(2)}, u32[]{:S(2)}) collective-permute-start(bf16[3,144,128]{2,1,0:T(8,128)(2,1)S(1)} %pad_maximum_fusion.1), channel_id=1, source_target_pairs={{0,6},{2,4},{4,2},{6,0},{1,7},{3,5},{5,3},{7,1},{8,14},{10,12},{12... | collective-permute-start | bytes 331784 | tf_op jit(solution)/shard_map/ppermute | solution.py:527
  26.7 2.2 %collective-permute-start.6 = (bf16[400,128]{1,0:T(8,128)(2,1)S(1)}, bf16[400,128]{1,0:T(8,128)(2,1)S(1)}, u32[]{:S(2)}, u32[]{:S(2)}) collective-permute-start(bf16[400,128]{1,0:T(8,128)(2,1)S(1)} %get-tuple-element.76), channel_id=1, source_target_pairs={{0,8},{8,0},{16,24},{24,16},{1,9},{9,1},{17,25},{25,17},{2,10},{10... | collective-permute-start | bytes 307208 | tf_op jit(solution)/shard_map/ppermute | solution.py:589
  26.8 4.7 %collective-permute-start.7 = (bf16[400,128]{1,0:T(8,128)(2,1)S(1)}, bf16[400,128]{1,0:T(8,128)(2,1)S(1)}, u32[]{:S(2)}, u32[]{:S(2)}) collective-permute-start(bf16[400,128]{1,0:T(8,128)(2,1)S(1)} %get-tuple-element.77), channel_id=1, source_target_pairs={{0,24},{8,16},{16,8},{24,0},{1,25},{9,17},{17,9},{25,1},{2,26},{10... | collective-permute-start | bytes 307208 | tf_op jit(solution)/shard_map/ppermute | solution.py:588
  28.5 4.7 %collective-permute-start.9 = (bf16[144,128]{1,0:T(8,128)(2,1)S(1)}, bf16[144,128]{1,0:T(8,128)(2,1)S(1)}, u32[]{:S(2)}, u32[]{:S(2)}) collective-permute-start(bf16[144,128]{1,0:T(8,128)(2,1)S(1)} %get-tuple-element.78), channel_id=1, source_target_pairs={{0,16},{8,24},{16,0},{24,8},{1,17},{9,25},{17,1},{25,9},{2,18},{10... | collective-permute-start | bytes 110600 | tf_op jit(solution)/shard_map/ppermute | solution.py:591
  31.6 6.2 %collective-permute-start.8 = (bf16[144,128]{1,0:T(8,128)(2,1)S(1)}, bf16[144,128]{1,0:T(8,128)(2,1)S(1)}, u32[]{:S(2)}, u32[]{:S(2)}) collective-permute-start(bf16[144,128]{1,0:T(8,128)(2,1)S(1)} %pad_maximum_fusion.5), channel_id=1, source_target_pairs={{0,6},{2,4},{4,2},{6,0},{1,7},{3,5},{5,3},{7,1},{8,14},{10,12},{12... | collective-permute-start | bytes 110600 | tf_op jit(solution)/shard_map/ppermute | solution.py:617
  33.2 5.5 %collective-permute-start.10 = (bf16[288,128]{1,0:T(8,128)(2,1)S(1)}, bf16[288,128]{1,0:T(8,128)(2,1)S(1)}, u32[]{:S(2)}, u32[]{:S(2)}) collective-permute-start(bf16[288,128]{1,0:T(8,128)(2,1)S(1)} %pad_maximum_fusion.4), channel_id=1, source_target_pairs={{0,2},{2,0},{4,6},{6,4},{1,3},{3,1},{5,7},{7,5},{8,10},{10,8},{12,... | collective-permute-start | bytes 221192 | tf_op jit(solution)/shard_map/ppermute | solution.py:614
  34.2 7.4 %collective-permute-start.5 = (bf16[288,128]{1,0:T(8,128)(2,1)S(1)}, bf16[288,128]{1,0:T(8,128)(2,1)S(1)}, u32[]{:S(2)}, u32[]{:S(2)}) collective-permute-start(bf16[288,128]{1,0:T(8,128)(2,1)S(1)} %get-tuple-element.97), channel_id=1, source_target_pairs={{0,24},{8,16},{16,8},{24,0},{1,25},{9,17},{17,9},{25,1},{2,26},{10... | collective-permute-start | bytes 221192 | tf_op jit(solution)/shard_map/ppermute | solution.py:620
  35.6 5.9 %collective-permute-start.4 = (bf16[288,128]{1,0:T(8,128)(2,1)S(1)}, bf16[288,128]{1,0:T(8,128)(2,1)S(1)}, u32[]{:S(2)}, u32[]{:S(2)}) collective-permute-start(bf16[288,128]{1,0:T(8,128)(2,1)S(1)} %get-tuple-element.98), channel_id=1, source_target_pairs={{0,8},{8,0},{16,24},{24,16},{1,9},{9,1},{17,25},{25,17},{2,10},{10... | collective-permute-start | bytes 221192 | tf_op jit(solution)/shard_map/ppermute | solution.py:621
  38.7 2.9 %collective-permute-start.11 = (bf16[32,128]{1,0:T(8,128)(2,1)S(1)}, bf16[32,128]{1,0:T(8,128)(2,1)S(1)}, u32[]{:S(2)}, u32[]{:S(2)}) collective-permute-start(bf16[32,128]{1,0:T(8,128)(2,1)S(1)} %pad_maximum_fusion.6), channel_id=1, source_target_pairs={{0,8},{8,0},{16,24},{24,16},{1,9},{9,1},{17,25},{25,17},{2,10},{10... | collective-permute-start | bytes 24584 | tf_op jit(solution)/shard_map/ppermute | solution.py:630
  38.8 3.1 %collective-permute-start.12 = (bf16[32,128]{1,0:T(8,128)(2,1)S(1)}, bf16[32,128]{1,0:T(8,128)(2,1)S(1)}, u32[]{:S(2)}, u32[]{:S(2)}) collective-permute-start(bf16[32,128]{1,0:T(8,128)(2,1)S(1)} %pad_maximum_fusion.6), channel_id=1, source_target_pairs={{0,24},{8,16},{16,8},{24,0},{1,25},{9,17},{17,9},{25,1},{2,26},{10... | collective-permute-start | bytes 24584 | tf_op jit(solution)/shard_map/ppermute | solution.py:629
  40.5 4.9 %collective-permute-start.13 = (bf16[144,128]{1,0:T(8,128)(2,1)S(1)}, bf16[144,128]{1,0:T(8,128)(2,1)S(1)}, u32[]{:S(2)}, u32[]{:S(2)}) collective-permute-start(bf16[144,128]{1,0:T(8,128)(2,1)S(1)} %add_convert_fusion), channel_id=1, source_target_pairs={{0,4},{2,6},{4,0},{6,2},{1,5},{3,7},{5,1},{7,3},{8,12},{10,14},{12... | collective-permute-start | bytes 110600 | tf_op jit(solution)/shard_map/ppermute | solution.py:626
  45.4 1.5 %collective-permute-start.14 = (f32[144,128]{1,0:T(8,128)S(1)}, f32[144,128]{1,0:T(8,128)S(1)}, u32[]{:S(2)}, u32[]{:S(2)}) collective-permute-start(f32[144,128]{1,0:T(8,128)S(1)} %convert_add_fusion.mine), channel_id=1, source_target_pairs={{0,8},{8,0},{16,24},{24,16},{1,9},{9,1},{17,25},{25,17},{2,10},{10... | collective-permute-start | bytes 221192 | tf_op jit(solution)/shard_map/ppermute | solution.py:640
